TPU v7x, 32 devices: a whole 2x2x4 slice. The times are simulated.
32 devices in a mesh: segment: 4 (over x, core), seq: 2 (over y), rep: 4 (over z).
Axes of the slice: x: 2, y: 2, z: 4, core: 2. Of those that a mesh axis runs over, the one named last changes fastest.
Arguments:
- query: bfloat16 [4, 384, 5120], P('segment', ('rep', 'seq')), parts along dimension 1, may hold values from -7 to 7
- key_new: bfloat16 [4, 384, 5120], P('segment', ('rep', 'seq')), parts along dimension 1, may hold values from -4 to 4
- value_new: bfloat16 [4, 384, 5120], P('segment', ('rep', 'seq')), parts along dimension 1, may hold values from -4 to 4
- stale_key: bfloat16 [4, 160, 192, 128], P('segment', ('rep', 'seq')), parts along dimension 1, may hold values from -12 to 12
- stale_value: bfloat16 [4, 160, 192, 128], P('segment', ('rep', 'seq')), parts along dimension 1, may hold values from -4 to 4
- head_order: int32 [40], replicated, may hold values from 0 to 39, each once
- tick: int32 [1], replicated, may hold values from 0 to 8191
Outputs:
- handoff: bfloat16 [4, 384, 5120], P('segment', ('rep', 'seq')), parts along dimension 1
There are 4 independent parts, one for each index of `rep`. A program takes and returns all parts, laid end to end along the dimension named above; an argument that names none is the same for every part. Nothing has to cross between parts.
Inputs may be any that keep to these rules, and one draw needn't show every extreme that they name: `head_order`: every head appears once. `tick`: only its value modulo 2 matters.
All inputs are finite; a program needn't handle non-finite values.
Results may differ from a plain program's by a relative error of at most 0.0044.
Values may be sent and summed in bfloat16 or wider, within the bound.
No kernel may reach another device: no remote copies, remote signals or barrier semaphores. Data moves between devices by JAX's collectives and lax.ppermute only.
A program may use at most 64 MiB of HBM per device.

v0:
```python
import jax
import jax.numpy as jnp
from jax import lax
from jax.sharding import PartitionSpec as P

MICRO = 2


def from_behind(block, axis, distance):
    devices = range(lax.axis_size(axis))
    route = [((i - distance) % len(devices), i) for i in devices]
    return lax.ppermute(block, axis, route)


def select_table(head_order, group_size, heads_dev):
    head_count = head_order.shape[0]
    slot_ids = (
        jnp.arange(heads_dev, dtype=jnp.int32)[None, :] * group_size
        + jnp.arange(group_size, dtype=jnp.int32)[:, None]
    )
    head_ids = jnp.arange(head_count, dtype=jnp.int32)
    matches = slot_ids[:, :, None] == head_ids[None, None, :]
    head_of = jnp.sum(jnp.where(matches, head_order[None, None, :], 0), axis=-1)
    head_of = jnp.where(slot_ids < head_count, head_of, -1)
    return (head_of[:, :, None] == head_ids[None, None, :]).astype(jnp.bfloat16)


def pack_heads(table, values, head_size):
    rows = values.shape[1]
    per_head = values[0].reshape(rows, table.shape[2], head_size)
    return jnp.einsum("dlh,thc->tdlc", table, per_head, preferred_element_type=jnp.float32).astype(
        jnp.bfloat16
    )


def head_major(received):
    return jnp.transpose(received[:, 0], (1, 0, 2))


def block_count(patch_tok):
    count = max(1, patch_tok // 512)
    while patch_tok % count != 0:
        count = count - 1
    return count


def per_device(query, key_new, value_new, stale_key, stale_value, head_order, tick):
    group_size = lax.axis_size("seq")
    heads_dev = stale_key.shape[1]
    head_size = stale_key.shape[3]
    tok_rows = query.shape[1]
    patch_tok = tok_rows * group_size
    blocks = block_count(patch_tok)
    block_rows = patch_tok // blocks
    score_scale = head_size ** (-0.5)
    table = select_table(head_order, group_size, heads_dev)
    patch_index = (tick[0] - lax.axis_index("segment")) % MICRO
    first_row = patch_index * patch_tok

    def with_fresh(stale_buf, fresh_rows):
        return lax.dynamic_update_slice(
            stale_buf[0], fresh_rows, (jnp.int32(0), first_row, jnp.int32(0))
        )

    sent_query, sent_key, sent_value = (
        lax.all_to_all(
            pack_heads(table, query, head_size), "seq", split_axis=1, concat_axis=0, tiled=True
        ),
        lax.all_to_all(
            pack_heads(table, key_new, head_size), "seq", split_axis=1, concat_axis=0, tiled=True
        ),
        lax.all_to_all(
            pack_heads(table, value_new, head_size), "seq", split_axis=1, concat_axis=0, tiled=True
        ),
    )
    key_buf = with_fresh(stale_key, head_major(sent_key))
    value_buf = with_fresh(stale_value, head_major(sent_value))

    def attend_full(operands):
        query_blocks, key_rows, value_rows = operands

        def one_block(query_rows):
            scores = (
                jnp.dot(query_rows, key_rows.T, preferred_element_type=jnp.float32) * score_scale
            )
            top = jnp.max(scores, axis=-1, keepdims=True)
            weights = jnp.exp(scores - top).astype(jnp.bfloat16)
            total = jnp.sum(weights, axis=-1, keepdims=True, dtype=jnp.float32)
            numer = jnp.dot(weights, value_rows, preferred_element_type=jnp.float32)
            return (numer / total).astype(jnp.bfloat16)

        return lax.map(one_block, query_blocks).reshape(patch_tok, head_size)

    heads_rows = head_major(sent_query)
    attended = lax.map(
        attend_full,
        (
            heads_rows.reshape(heads_rows.shape[0], blocks, block_rows, heads_rows.shape[-1]),
            key_buf,
            value_buf,
        ),
    )
    outgoing = jnp.transpose(attended, (1, 0, 2))[:, None, :, :]
    returned = lax.all_to_all(outgoing, "seq", split_axis=0, concat_axis=1, tiled=True)
    merged = jnp.einsum(
        "dlh,tdlc->thc", table, returned, preferred_element_type=jnp.float32
    ).astype(jnp.bfloat16)
    result = merged.reshape(1, tok_rows, table.shape[2] * head_size)
    return from_behind(result, "segment", 1)


def solution(mesh):
    return jax.shard_map(
        per_device,
        mesh=mesh,
        in_specs=(
            P("segment", ("rep", "seq"), None),
            P("segment", ("rep", "seq"), None),
            P("segment", ("rep", "seq"), None),
            P("segment", ("rep", "seq"), None, None),
            P("segment", ("rep", "seq"), None, None),
            P(),
            P(),
        ),
        out_specs=P("segment", ("rep", "seq"), None),
        check_vma=False,
    )
```

profile of v0, /device:TPU:0, one launch (start us, length us, event | category | flops | bytes accessed | tf_op | source)
XLA Modules:
  0.0 69.6 jit_solution(15372315159979951298)
XLA Ops:
  0.1 0.6 copy-done.6
  0.7 0.5 fusion.24
  1.4 0.4 fusion.13
  1.8 0.8 %copy.34 = bf16[48,2,20,128]{3,0,2,1:T(8,128)(2,1)} copy(bf16[48,2,20,128]{3,2,0,1:T(8,128)(2,1)S(1)} %fusion.13) | data formatting | bytes 983040 | tf_op jit(solution)/shard_map/convert_element_type | solution.py:31
  2.6 4.2 %all-to-all-start.1 = ((bf16[48,2,20,128]{3,0,2,1:T(8,128)(2,1)}), bf16[48,2,20,128]{3,0,2,1:T(8,128)(2,1)S(1)}, u32[]{:S(2)}, u32[]{:S(2)}) async-start(bf16[48,2,20,128]{3,0,2,1:T(8,128)(2,1)} %copy.34), calls=%async_computation.1 | async-start | bytes 983040 | tf_op jit(solution)/shard_map/all_to_all | solution.py:69
  6.9 0.4 fusion.14
  7.3 0.8 %copy.36 = bf16[48,2,20,128]{3,0,2,1:T(8,128)(2,1)} copy(bf16[48,2,20,128]{3,2,0,1:T(8,128)(2,1)S(1)} %fusion.14) | data formatting | bytes 983040 | tf_op jit(solution)/shard_map/convert_element_type | solution.py:31
  8.2 7.0 %all-to-all-done.1 = bf16[48,2,20,128]{3,0,2,1:T(8,128)(2,1)S(1)} async-done(((bf16[48,2,20,128]{3,0,2,1:T(8,128)(2,1)}), bf16[48,2,20,128]{3,0,2,1:T(8,128)(2,1)S(1)}, u32[]{:S(2)}, u32[]{:S(2)}) %all-to-all-start.1) | async-done | bytes 491552 | tf_op jit(solution)/shard_map/all_to_all | solution.py:69
  15.2 3.5 %all-to-all-start.2 = ((bf16[48,2,20,128]{3,0,2,1:T(8,128)(2,1)}), bf16[48,2,20,128]{3,0,2,1:T(8,128)(2,1)S(1)}, u32[]{:S(2)}, u32[]{:S(2)}) async-start(bf16[48,2,20,128]{3,0,2,1:T(8,128)(2,1)} %copy.36), calls=%async_computation.2 | async-start | bytes 983040 | tf_op jit(solution)/shard_map/all_to_all | solution.py:72
  18.7 0.4 fusion.12
  19.1 0.8 %copy.32 = bf16[48,2,20,128]{3,0,2,1:T(8,128)(2,1)} copy(bf16[48,2,20,128]{3,2,0,1:T(8,128)(2,1)S(1)} %fusion.12) | data formatting | bytes 983040 | tf_op jit(solution)/shard_map/convert_element_type | solution.py:31
  19.9 6.1 %all-to-all-done.2 = bf16[48,2,20,128]{3,0,2,1:T(8,128)(2,1)S(1)} async-done(((bf16[48,2,20,128]{3,0,2,1:T(8,128)(2,1)}), bf16[48,2,20,128]{3,0,2,1:T(8,128)(2,1)S(1)}, u32[]{:S(2)}, u32[]{:S(2)}) %all-to-all-start.2) | async-done | bytes 491552 | tf_op jit(solution)/shard_map/all_to_all | solution.py:72
  26.0 3.5 %all-to-all-start = ((bf16[48,2,20,128]{3,0,2,1:T(8,128)(2,1)}), bf16[48,2,20,128]{3,0,2,1:T(8,128)(2,1)S(1)}, u32[]{:S(2)}, u32[]{:S(2)}) async-start(bf16[48,2,20,128]{3,0,2,1:T(8,128)(2,1)} %copy.32), calls=%async_computation | async-start | bytes 983040 | tf_op jit(solution)/shard_map/all_to_all | solution.py:66
  30.3 1.1 %copy-done = bf16[1,20,192,128]{3,2,1,0:T(8,128)(2,1)S(1)} copy-done((bf16[1,20,192,128]{3,2,1,0:T(8,128)(2,1)S(1)}, bf16[1,20,192,128]{3,2,1,0:T(8,128)(2,1)}, u32[]{:S(2)}) %copy-start) | copy-done | bytes 983064
  31.4 0.3 copy-done.1
  31.9 4.1 %all-to-all-done = bf16[48,2,20,128]{3,0,2,1:T(8,128)(2,1)S(1)} async-done(((bf16[48,2,20,128]{3,0,2,1:T(8,128)(2,1)}), bf16[48,2,20,128]{3,0,2,1:T(8,128)(2,1)S(1)}, u32[]{:S(2)}, u32[]{:S(2)}) %all-to-all-start) | async-done | bytes 491552 | tf_op jit(solution)/shard_map/all_to_all | solution.py:66
  36.0 14.3 %while.10 = (s32[]{:T(128)}, bf16[20,96,128]{2,1,0:T(8,128)(2,1)S(1)}, bf16[20,1,96,128]{3,2,1,0:T(8,128)(2,1)S(1)}, bf16[20,192,128]{2,1,0:T(8,128)(2,1)S(1)}, bf16[20,192,128]{2,1,0:T(8,128)(2,1)S(1)}, /*index=5*/s32[]{:T(128)}) while((s32[]{:T(128)}, bf16[20,96,128]{2,1,0:T(8,128)(2,1)S(1)}, bf16[20,1,96,128]{3,2,1,0:T(8,128)(2,1)S(1)}, ...), condition=%wide.region_4.5_spmd, body=%wide.region_1.4_spmd.sunk | while | flops 9609026 | bytes 397509 | solution.py:95
  36.0 0.3 fusion.37
  36.7 0.3 fusion.37
  37.4 0.3 fusion.37
  38.1 0.3 fusion.37
  38.9 0.3 fusion.37
  39.6 0.3 fusion.37
  40.3 0.3 fusion.37
  41.7 0.3 fusion.37
  42.4 0.3 fusion.37
  43.1 0.3 fusion.37
  43.9 0.3 fusion.37
  50.5 9.3 %all_to_all.63 = bf16[96,1,20,128]{3,2,1,0:T(8,128)(2,1)S(1)} all-to-all(bf16[96,1,20,128]{3,2,1,0:T(8,128)(2,1)S(1)} %bitcast.108), channel_id=1, replica_groups=mesh['segment'=4,'seq'=2,'rep'=4] {'seq'}, dimensions={0} | all-to-all | bytes 983040 | tf_op jit(solution)/shard_map/all_to_all | solution.py:104
  59.9 0.4 fusion.15
  60.6 8.2 %collective-permute-done = bf16[1,48,5120]{2,1,0:T(8,128)(2,1)S(1)} collective-permute-done((bf16[1,48,5120]{2,1,0:T(8,128)(2,1)S(1)}, bf16[1,48,5120]{2,1,0:T(8,128)(2,1)S(1)}, u32[]{:S(2)}, u32[]{:S(2)}) %collective-permute-start) | collective-permute-done | bytes 491552 | tf_op jit(solution)/shard_map/ppermute | solution.py:12
  68.8 0.8 %copy.72 = bf16[1,48,5120]{2,1,0:T(8,128)(2,1)} copy(bf16[1,48,5120]{2,1,0:T(8,128)(2,1)S(1)} %collective-permute-done) | data formatting | bytes 983040
  (75 shorter events, 11.9 us)
Async XLA Ops:
  0.0 0.7 copy-start.6
  0.0 1.3 %copy-start.2 = (bf16[1,48,5120]{2,1,0:T(8,128)(2,1)S(1)}, bf16[1,48,5120]{2,1,0:T(8,128)(2,1)}, u32[]{:S(2)}) copy-start(bf16[1,48,5120]{2,1,0:T(8,128)(2,1)} %param.10) | copy-start | bytes 1474564
  1.8 5.1 %copy-start.3 = (bf16[1,48,5120]{2,1,0:T(8,128)(2,1)S(1)}, bf16[1,48,5120]{2,1,0:T(8,128)(2,1)}, u32[]{:S(2)}) copy-start(bf16[1,48,5120]{2,1,0:T(8,128)(2,1)} %param.11) | copy-start | bytes 1474564
  2.6 12.6 %all-to-all-start.1 = ((bf16[48,2,20,128]{3,0,2,1:T(8,128)(2,1)}), bf16[48,2,20,128]{3,0,2,1:T(8,128)(2,1)S(1)}, u32[]{:S(2)}, u32[]{:S(2)}) async-start(bf16[48,2,20,128]{3,0,2,1:T(8,128)(2,1)} %copy.34), calls=%async_computation.1 | async-start | bytes 983040 | tf_op jit(solution)/shard_map/all_to_all | solution.py:69
  6.9 1.2 %copy-start.4 = (bf16[1,48,5120]{2,1,0:T(8,128)(2,1)S(1)}, bf16[1,48,5120]{2,1,0:T(8,128)(2,1)}, u32[]{:S(2)}) copy-start(bf16[1,48,5120]{2,1,0:T(8,128)(2,1)} %param.9) | copy-start | bytes 1474564
  15.2 10.8 %all-to-all-start.2 = ((bf16[48,2,20,128]{3,0,2,1:T(8,128)(2,1)}), bf16[48,2,20,128]{3,0,2,1:T(8,128)(2,1)S(1)}, u32[]{:S(2)}, u32[]{:S(2)}) async-start(bf16[48,2,20,128]{3,0,2,1:T(8,128)(2,1)} %copy.36), calls=%async_computation.2 | async-start | bytes 983040 | tf_op jit(solution)/shard_map/all_to_all | solution.py:72
  26.0 9.9 %all-to-all-start = ((bf16[48,2,20,128]{3,0,2,1:T(8,128)(2,1)}), bf16[48,2,20,128]{3,0,2,1:T(8,128)(2,1)S(1)}, u32[]{:S(2)}, u32[]{:S(2)}) async-start(bf16[48,2,20,128]{3,0,2,1:T(8,128)(2,1)} %copy.32), calls=%async_computation | async-start | bytes 983040 | tf_op jit(solution)/shard_map/all_to_all | solution.py:66
  30.2 1.2 %copy-start = (bf16[1,20,192,128]{3,2,1,0:T(8,128)(2,1)S(1)}, bf16[1,20,192,128]{3,2,1,0:T(8,128)(2,1)}, u32[]{:S(2)}) copy-start(bf16[1,20,192,128]{3,2,1,0:T(8,128)(2,1)} %param.12) | copy-start | bytes 2949124
  30.2 1.5 %copy-start.1 = (bf16[1,20,192,128]{3,2,1,0:T(8,128)(2,1)S(1)}, bf16[1,20,192,128]{3,2,1,0:T(8,128)(2,1)}, u32[]{:S(2)}) copy-start(bf16[1,20,192,128]{3,2,1,0:T(8,128)(2,1)} %param.13) | copy-start | bytes 2949124
  31.8 4.1 %copy-start.5 = (bf16[20,96,128]{2,1,0:T(8,128)(2,1)S(1)}, bf16[20,96,128]{2,1,0:T(8,128)(2,1)}, u32[]{:S(2)}) copy-start(bf16[20,96,128]{2,1,0:T(8,128)(2,1)} %custom-call) | copy-start | bytes 1474564
  60.5 8.3 %collective-permute-start = (bf16[1,48,5120]{2,1,0:T(8,128)(2,1)S(1)}, bf16[1,48,5120]{2,1,0:T(8,128)(2,1)S(1)}, u32[]{:S(2)}, u32[]{:S(2)}) collective-permute-start(bf16[1,48,5120]{2,1,0:T(8,128)(2,1)S(1)} %reshape.60), channel_id=1, source_target_pairs={{24,0},{0,8},{8,16},{16,24},{25,1},{1,9},{9,17},{17,25},{26,2},{2,... | collective-permute-start | bytes 1474568 | tf_op jit(solution)/shard_map/ppermute | solution.py:12
where the time goes:
time: 70 us; the launch traced here: 69.6 us
  waiting for transfers between devices  25.4 us (36%)
  matrix products  11.4 us (16%)
  starting transfers between devices  11.3 us (16%)
  blocking collectives  9.35 us (13%)
  local copies, waits for them, and re-layouts  6.24 us (9%)
  other arithmetic  4.44 us (6%)
  between operations  0.87 us (1%)
    all_to_all x1, blocking collectives, per_device(): lax.all_to_all(outgoing, 'seq', split_axis=0, concat_axis=1, tiled=True)  9.35 us
    ppermute x1, waiting for transfers between devices, from_behind(): return lax.ppermute(block, axis, route)  8.24 us
    all_to_all x1, waiting for transfers between devices, per_device(): lax.all_to_all(pack_heads(table, key_new, head_size), 'seq', split_axis=1...  7 us
    all_to_all x1, waiting for transfers between devices, per_device(): lax.all_to_all(pack_heads(table, value_new, head_size), 'seq', split_axis...  6.12 us
    dot_general x20, matrix products, one_block(): jnp.dot(query_rows, key_rows.T, preferred_element_type=jnp.float32)  5.46 us
    dot_general x20, matrix products, one_block(): numer = jnp.dot(weights, value_rows, preferred_element_type=jnp.float32)  4.42 us
    all_to_all x1, starting transfers between devices, per_device(): lax.all_to_all(pack_heads(table, key_new, head_size), 'seq', split_axis=1...  4.23 us
    all_to_all x1, waiting for transfers between devices, per_device(): lax.all_to_all(pack_heads(table, query, head_size), 'seq', split_axis=1,...  4.07 us
  transfers between devices with their start and end apart: 4, of which 4 were waited for; matrix products, arithmetic and copies ran while one was open for 4% of the time, Pallas kernels for 0%

commit v1 on v0

--- a/solution.py
+++ b/solution.py
@@ -1,9 +1,15 @@
+import functools
+
 import jax
 import jax.numpy as jnp
 from jax import lax
+from jax.experimental import pallas as pl
+from jax.experimental.pallas import tpu as pltpu
 from jax.sharding import PartitionSpec as P
 
 MICRO = 2
+CHUNKS = 1
+KERNEL_VMEM = 16 << 20
 
 
 def from_behind(block, axis, distance):
@@ -44,7 +50,7 @@
     return count
 
 
-def per_device(query, key_new, value_new, stale_key, stale_value, head_order, tick):
+def wide_group(query, key_new, value_new, stale_key, stale_value, head_order, tick):
     group_size = lax.axis_size("seq")
     heads_dev = stale_key.shape[1]
     head_size = stale_key.shape[3]
@@ -64,14 +70,9 @@
 
     sent_query, sent_key, sent_value = (
         lax.all_to_all(
-            pack_heads(table, query, head_size), "seq", split_axis=1, concat_axis=0, tiled=True
-        ),
-        lax.all_to_all(
-            pack_heads(table, key_new, head_size), "seq", split_axis=1, concat_axis=0, tiled=True
-        ),
-        lax.all_to_all(
-            pack_heads(table, value_new, head_size), "seq", split_axis=1, concat_axis=0, tiled=True
-        ),
+            pack_heads(table, part, head_size), "seq", split_axis=1, concat_axis=0, tiled=True
+        )
+        for part in (query, key_new, value_new)
     )
     key_buf = with_fresh(stale_key, head_major(sent_key))
     value_buf = with_fresh(stale_value, head_major(sent_value))
@@ -107,6 +108,212 @@
     ).astype(jnp.bfloat16)
     result = merged.reshape(1, tok_rows, table.shape[2] * head_size)
     return from_behind(result, "segment", 1)
+
+
+def any_space():
+    return pl.BlockSpec(memory_space=pl.ANY)
+
+
+def scalar_space():
+    return pl.BlockSpec(memory_space=pltpu.SMEM)
+
+
+def columns_of(order_ref, unit, head_size):
+    return pl.ds(pl.multiple_of(order_ref[unit] * head_size, head_size), head_size)
+
+
+def pack_body(low, heads, order_ref, query_ref, key_ref, value_ref, out_ref, sem):
+    other = 1 - lax.axis_index("seq")
+    head_size = out_ref.shape[3]
+    for l in range(heads):
+        columns = columns_of(order_ref, 2 * (low + l) + other, head_size)
+        for place, source in enumerate((key_ref, value_ref, query_ref)):
+            pltpu.make_async_copy(source.at[0, :, columns], out_ref.at[place, l], sem).start()
+    pltpu.make_async_copy(out_ref, out_ref, sem).wait()
+
+
+def pack(low, heads, head_order, query, key_new, value_new):
+    tok_rows = query.shape[1]
+    head_size = query.shape[2] // head_order.shape[0]
+    shape = (3, heads, tok_rows, head_size)
+    return pl.pallas_call(
+        functools.partial(pack_body, low, heads),
+        out_shape=jax.ShapeDtypeStruct(shape, query.dtype),
+        in_specs=[scalar_space()] + [any_space()] * 3,
+        out_specs=any_space(),
+        scratch_shapes=[pltpu.SemaphoreType.DMA],
+        cost_estimate=pl.CostEstimate(
+            flops=0, bytes_accessed=12 * heads * tok_rows * head_size, transcendentals=0
+        ),
+        compiler_params=pltpu.CompilerParams(vmem_limit_bytes=KERNEL_VMEM),
+        name="pack",
+    )(head_order, query, key_new, value_new)
+
+
+def attend_body(
+    low,
+    heads,
+    order_ref,
+    tick_ref,
+    query_ref,
+    key_ref,
+    value_ref,
+    recv_ref,
+    stale_key_ref,
+    stale_value_ref,
+    near_ref,
+    far_ref,
+    query_buf,
+    key_buf,
+    value_buf,
+    sems,
+):
+    me = lax.axis_index("seq")
+    tok_rows, head_size = near_ref.shape[1:]
+    patch_tok = 2 * tok_rows
+    kept = (tick_ref[0] - lax.axis_index("segment") + 1) & 1
+    kept_rows = pl.ds(pl.multiple_of(kept * patch_tok, patch_tok), patch_tok)
+    group = pl.ds(low, heads)
+    columns = pl.ds(0, head_size)
+    own = pl.ds(patch_tok, tok_rows)
+    got = pl.ds(patch_tok + tok_rows, tok_rows)
+    key_sem, value_sem, query_sem = sems.at[0], sems.at[1], sems.at[2]
+
+    pltpu.make_async_copy(
+        stale_key_ref.at[0, group, kept_rows], key_buf.at[:, pl.ds(0, patch_tok)], key_sem
+    ).start()
+    pltpu.make_async_copy(
+        stale_value_ref.at[0, group, kept_rows],
+        value_buf.at[:, pl.ds(0, patch_tok), columns],
+        value_sem,
+    ).start()
+    pltpu.make_async_copy(recv_ref.at[0], key_buf.at[:, got], key_sem).start()
+    pltpu.make_async_copy(recv_ref.at[1], value_buf.at[:, got, columns], value_sem).start()
+    pltpu.make_async_copy(
+        recv_ref.at[2], query_buf.at[:, pl.ds(tok_rows, tok_rows)], query_sem
+    ).start()
+    for l in range(heads):
+        head = columns_of(order_ref, 2 * (low + l) + me, head_size)
+        pltpu.make_async_copy(key_ref.at[0, :, head], key_buf.at[l, own], key_sem).start()
+        pltpu.make_async_copy(
+            query_ref.at[0, :, head], query_buf.at[l, pl.ds(0, tok_rows)], query_sem
+        ).start()
+        pltpu.make_async_copy(
+            value_ref.at[0, :, head], value_buf.at[l, own, columns], value_sem
+        ).start()
+    value_buf[:, :, head_size:] = jnp.ones(
+        (heads, value_buf.shape[1], head_size), value_buf.dtype
+    )
+    pltpu.make_async_copy(query_buf, query_buf, query_sem).wait()
+    pltpu.make_async_copy(key_buf, key_buf, key_sem).wait()
+    pltpu.make_async_copy(
+        value_buf.at[:, :, columns], value_buf.at[:, :, columns], value_sem
+    ).wait()
+
+    factor = head_size ** (-0.5) * 1.4426950408889634
+    for l in range(heads):
+        scores = lax.dot_general(
+            query_buf[l], key_buf[l], (((1,), (1,)), ((), ())), preferred_element_type=jnp.float32
+        )
+        top = jnp.max(scores, axis=-1, keepdims=True)
+        weights = jnp.exp2((scores - top) * factor).astype(jnp.bfloat16)
+        both = jnp.dot(weights, value_buf[l], preferred_element_type=jnp.float32)
+        result = (both[:, :head_size] / both[:, head_size:]).astype(near_ref.dtype)
+        near_ref[l] = result[:tok_rows]
+        far_ref[l] = result[tok_rows:]
+
+
+def attend(low, heads, head_order, tick, query, key_new, value_new, received, stale_key, stale_value):
+    tok_rows = query.shape[1]
+    length, head_size = stale_key.shape[2:]
+    out = jax.ShapeDtypeStruct((heads, tok_rows, head_size), query.dtype)
+    return pl.pallas_call(
+        functools.partial(attend_body, low, heads),
+        out_shape=(out, out),
+        in_specs=[scalar_space()] * 2 + [any_space()] * 6,
+        out_specs=(pl.BlockSpec(memory_space=pltpu.VMEM),) * 2,
+        scratch_shapes=[
+            pltpu.VMEM((heads, 2 * tok_rows, head_size), query.dtype),
+            pltpu.VMEM((heads, length, head_size), query.dtype),
+            pltpu.VMEM((heads, length, 2 * head_size), query.dtype),
+            pltpu.SemaphoreType.DMA((3,)),
+        ],
+        cost_estimate=pl.CostEstimate(
+            flops=12 * heads * tok_rows * length * head_size,
+            bytes_accessed=2 * heads * head_size * (2 * length + 4 * tok_rows),
+            transcendentals=2 * heads * tok_rows * length,
+        ),
+        compiler_params=pltpu.CompilerParams(vmem_limit_bytes=KERNEL_VMEM),
+        name="attend",
+    )(head_order, tick, query, key_new, value_new, received, stale_key, stale_value)
+
+
+def unpack_body(bounds, order_ref, *refs):
+    count = len(bounds)
+    near, far = refs[:count], refs[count : 2 * count]
+    out_ref, sem = refs[2 * count :]
+    me = lax.axis_index("seq")
+    head_size = near[0].shape[2]
+    for c, (low, heads) in enumerate(bounds):
+        for l in range(heads):
+            for side, source in ((me, near[c]), (1 - me, far[c])):
+                columns = columns_of(order_ref, 2 * (low + l) + side, head_size)
+                pltpu.make_async_copy(source.at[l], out_ref.at[0, :, columns], sem).start()
+    pltpu.make_async_copy(out_ref, out_ref, sem).wait()
+
+
+def unpack(bounds, head_order, near, far):
+    tok_rows, head_size = near[0].shape[1:]
+    shape = (1, tok_rows, head_order.shape[0] * head_size)
+    return pl.pallas_call(
+        functools.partial(unpack_body, bounds),
+        out_shape=jax.ShapeDtypeStruct(shape, near[0].dtype),
+        in_specs=[scalar_space()] + [any_space()] * (2 * len(bounds)),
+        out_specs=any_space(),
+        scratch_shapes=[pltpu.SemaphoreType.DMA],
+        cost_estimate=pl.CostEstimate(
+            flops=0, bytes_accessed=4 * shape[1] * shape[2], transcendentals=0
+        ),
+        compiler_params=pltpu.CompilerParams(vmem_limit_bytes=KERNEL_VMEM),
+        name="unpack",
+    )(head_order, *near, *far)
+
+
+def pair_group(query, key_new, value_new, stale_key, stale_value, head_order, tick):
+    heads_dev = stale_key.shape[1]
+    segments = lax.axis_size("segment")
+    edges = [heads_dev * c // CHUNKS for c in range(CHUNKS + 1)]
+    bounds = [(a, b - a) for a, b in zip(edges[:-1], edges[1:])]
+    ahead = [(s, (s + 1) % segments) for s in range(segments)]
+    across = [(2 * s + j, 2 * t + 1 - j) for s, t in ahead for j in range(2)]
+
+    received = []
+    for low, heads in bounds:
+        packed = pack(low, heads, head_order, query, key_new, value_new)
+        received.append(lax.ppermute(packed, "seq", [(0, 1), (1, 0)]))
+    near, far = [], []
+    for (low, heads), got in zip(bounds, received):
+        kept, crossed = attend(
+            low, heads, head_order, tick, query, key_new, value_new, got, stale_key, stale_value
+        )
+        far.append(lax.ppermute(crossed, ("segment", "seq"), across))
+        near.append(lax.ppermute(kept, "segment", ahead))
+    return unpack(bounds, head_order, near, far)
+
+
+def per_device(query, key_new, value_new, stale_key, stale_value, head_order, tick):
+    group_size = lax.axis_size("seq")
+    heads = head_order.shape[0]
+    tok_rows, head_size = query.shape[1], stale_key.shape[3]
+    paired = (
+        group_size == 2
+        and heads == 2 * stale_key.shape[1]
+        and stale_key.shape[2] == MICRO * 2 * tok_rows
+        and tok_rows % 16 == 0
+        and head_size % 128 == 0
+    )
+    chosen = pair_group if paired else wide_group
+    return chosen(query, key_new, value_new, stale_key, stale_value, head_order, tick)
 
 
 def solution(mesh):

time: 70 us -> 42 us (0.60)
  matrix products: 11.4 us -> 0 us
  blocking collectives: 9.35 us -> 0 us
  Pallas kernels: 0 us -> 8.77 us
  starting transfers between devices: 11.3 us -> 6.03 us
  other arithmetic: 4.44 us -> 0 us
  waiting for transfers between devices: 25.4 us -> 22.4 us
  local copies, waits for them, and re-layouts: 6.24 us -> 3.75 us
    all_to_all x3 -> x0, waiting for transfers between devices: 17.2 us -> none  [the longest x1 7 us: per_device(): lax.all_to_all(pack_heads(table, key_new, head_size), 'seq', split_axis=1...]
    ppermute x1 -> x3, waiting for transfers between devices: 8.24 us -> 22.4 us  [the longest x1 15.8 us: pair_group(): received.append(lax.ppermute(packed, 'seq', [(0, 1), (1, 0)]))]
    dot_general x44 -> x0, matrix products: 11.4 us -> none  [the longest x20 5.46 us: one_block(): jnp.dot(query_rows, key_rows.T, preferred_element_type=jnp.float32)]
    all_to_all x3 -> x0, starting transfers between devices: 11.2 us -> none  [the longest x1 4.23 us: per_device(): lax.all_to_all(pack_heads(table, key_new, head_size), 'seq', split_axis=1...]
    all_to_all x1 -> x0, blocking collectives: 9.35 us -> none  [per_device(): lax.all_to_all(outgoing, 'seq', split_axis=0, concat_axis=1, tiled=True)]
    pallas_call x0 -> x3, Pallas kernels: none -> 8.77 us  [the longest x1 6.55 us: attend(): pl.pallas_call(functools.partial(attend_body, low, heads), out_shape=(out...]
    ppermute x1 -> x3, starting transfers between devices: 0.06 us -> 6.03 us  [the longest x1 3.03 us: pair_group(): received.append(lax.ppermute(packed, 'seq', [(0, 1), (1, 0)]))]
    reduce_sum x21 -> x0, other arithmetic: 4.29 us -> none  [the longest x20 3.81 us: one_block(): total = jnp.sum(weights, axis=-1, keepdims=True, dtype=jnp.float32)]
  transfers between devices with their start and end apart: 4 -> 3, of which waited for: 4 -> 3; matrix products, arithmetic and copies ran while one was open for 4% -> 0% of each run, Pallas kernels for 0% -> 0%
where the time goes in v1:
time: 42 us; the launch traced here: 41.7 us
  waiting for transfers between devices  22.4 us (53%)
  Pallas kernels  8.77 us (21%)
  starting transfers between devices  6.03 us (14%)
  local copies, waits for them, and re-layouts  3.75 us (9%)
  between operations  0.68 us (2%)
    ppermute x1, waiting for transfers between devices, pair_group(): received.append(lax.ppermute(packed, 'seq', [(0, 1), (1, 0)]))  15.8 us
    pallas_call x1, Pallas kernels, attend(): pl.pallas_call(functools.partial(attend_body, low, heads), out_shape=(out...  6.55 us
    ppermute x1, waiting for transfers between devices, pair_group(): far.append(lax.ppermute(crossed, ('segment', 'seq'), across))  3.92 us
    unnamed x12, local copies, waits for them, and re-layouts  3.75 us
    ppermute x1, starting transfers between devices, pair_group(): received.append(lax.ppermute(packed, 'seq', [(0, 1), (1, 0)]))  3.03 us
    ppermute x1, starting transfers between devices, pair_group(): far.append(lax.ppermute(crossed, ('segment', 'seq'), across))  2.94 us
    ppermute x1, waiting for transfers between devices, pair_group(): near.append(lax.ppermute(kept, 'segment', ahead))  2.67 us
    pallas_call x1, Pallas kernels, unpack(): pl.pallas_call(functools.partial(unpack_body, bounds), out_shape=jax.Shap...  1.31 us
  transfers between devices with their start and end apart: 3, of which 3 were waited for; matrix products, arithmetic and copies ran while one was open for 0% of the time, Pallas kernels for 0%

profile of v1, /device:TPU:0, one launch (start us, length us, event | category | flops | bytes accessed | tf_op | source)
XLA Modules:
  0.0 41.7 jit_solution(12101667945558691192)
XLA Ops:
  0.0 0.0 copy-start
  0.0 1.0 %copy-done = bf16[1,48,5120]{2,1,0:T(8,128)(2,1)S(1)} copy-done((bf16[1,48,5120]{2,1,0:T(8,128)(2,1)S(1)}, bf16[1,48,5120]{2,1,0:T(8,128)(2,1)}, u32[]{:S(2)}) %copy-start) | copy-done | bytes 491544
  1.0 0.0 copy-start.1
  1.0 1.0 %copy-done.1 = bf16[1,48,5120]{2,1,0:T(8,128)(2,1)S(1)} copy-done((bf16[1,48,5120]{2,1,0:T(8,128)(2,1)S(1)}, bf16[1,48,5120]{2,1,0:T(8,128)(2,1)}, u32[]{:S(2)}) %copy-start.1) | copy-done | bytes 491544
  2.1 0.0 copy-start.2
  2.1 1.0 %copy-done.2 = bf16[1,48,5120]{2,1,0:T(8,128)(2,1)S(1)} copy-done((bf16[1,48,5120]{2,1,0:T(8,128)(2,1)S(1)}, bf16[1,48,5120]{2,1,0:T(8,128)(2,1)}, u32[]{:S(2)}) %copy-start.2) | copy-done | bytes 491544
  3.1 0.0 copy-start.5
  3.1 0.7 %copy-done.5 = s32[40]{0:T(128)S(1)} copy-done((s32[40]{0:T(128)S(1)}, s32[40]{0:T(128)}, u32[]{:S(2)}) %copy-start.5) | copy-done | bytes 184
  3.7 0.0 copy-start.3
  3.8 0.0 copy-start.4
  3.8 0.9 %pack.1 = bf16[3,20,48,128]{3,2,1,0:T(8,128)(2,1)S(1)} custom-call(s32[40]{0:T(128)S(1)} %copy-done.5, bf16[1,48,5120]{2,1,0:T(8,128)(2,1)S(1)} %copy-done, bf16[1,48,5120]{2,1,0:T(8,128)(2,1)S(1)} %copy-done.1, bf16[1,48,5120]{2,1,0:T(8,128)(2,1)S(1)} %copy-done.2), custom_call_target="tpu_custom_call" | custom-call | bytes 1474560 | tf_op jit(solution)/shard_map/pack/pallas_call | solution.py:139
  4.7 3.0 %collective-permute-start = (bf16[3,20,48,128]{3,2,1,0:T(8,128)(2,1)S(1)}, bf16[3,20,48,128]{3,2,1,0:T(8,128)(2,1)S(1)}, u32[]{:S(2)}, u32[]{:S(2)}) collective-permute-start(bf16[3,20,48,128]{3,2,1,0:T(8,128)(2,1)S(1)} %pack.1), channel_id=1, source_target_pairs={{0,4},{4,0},{1,5},{5,1},{2,6},{6,2},{3,7},{7,3},{8,12},{12,8},{9,1... | collective-permute-start | bytes 2211848 | tf_op jit(solution)/shard_map/ppermute | solution.py:293
  8.4 15.8 %collective-permute-done.recv_ref = bf16[3,20,48,128]{3,2,1,0:T(8,128)(2,1)S(1)} collective-permute-done((bf16[3,20,48,128]{3,2,1,0:T(8,128)(2,1)S(1)}, bf16[3,20,48,128]{3,2,1,0:T(8,128)(2,1)S(1)}, u32[]{:S(2)}, u32[]{:S(2)}) %collective-permute-start) | collective-permute-done | bytes 737312 | tf_op jit(solution)/shard_map/ppermute | solution.py:293
  24.2 0.0 copy-done.3
  24.2 0.0 copy-done.4
  24.2 6.5 %attend.1 = (bf16[20,48,128]{2,1,0:T(8,128)(2,1)S(1)}, bf16[20,48,128]{2,1,0:T(8,128)(2,1)S(1)}) custom-call(s32[40]{0:T(128)S(1)} %copy-done.5, s32[1]{0:T(128)S(6)} %copy.8.tick_ref, bf16[1,48,5120]{2,1,0:T(8,128)(2,1)S(1)} %copy-done, bf16[1,48,5120]{2,1,0:T(8,128)(2,1)S(1)} %copy-done.1, bf16[1,48,5120]{2,1,0:T(8,128)(2,1)S(1)} %copy-done.2, ...), custom_call_target="tpu_custom_call" | custom-call | flops 283115520 | bytes 2949120 | tf_op jit(solution)/shard_map/attend/pallas_call | solution.py:230
  30.8 0.1 collective-permute-start.1
  30.8 2.9 %collective-permute-start.2 = (bf16[20,48,128]{2,1,0:T(8,128)(2,1)S(1)}, bf16[20,48,128]{2,1,0:T(8,128)(2,1)S(1)}, u32[]{:S(2)}, u32[]{:S(2)}) collective-permute-start(bf16[20,48,128]{2,1,0:T(8,128)(2,1)S(1)} %get-tuple-element.8), channel_id=1, source_target_pairs={{0,12},{4,8},{8,20},{12,16},{16,28},{20,24},{24,4},{28,0},{1,13},{... | collective-permute-start | bytes 737288 | tf_op jit(solution)/shard_map/ppermute | solution.py:299
  33.8 2.7 %collective-permute-done.1.refs_0_ = bf16[20,48,128]{2,1,0:T(8,128)(2,1)S(1)} collective-permute-done((bf16[20,48,128]{2,1,0:T(8,128)(2,1)S(1)}, bf16[20,48,128]{2,1,0:T(8,128)(2,1)S(1)}, u32[]{:S(2)}, u32[]{:S(2)}) %collective-permute-start.1) | collective-permute-done | bytes 245792 | tf_op jit(solution)/shard_map/ppermute | solution.py:300
  36.4 3.9 %collective-permute-done.2.refs_1_ = bf16[20,48,128]{2,1,0:T(8,128)(2,1)S(1)} collective-permute-done((bf16[20,48,128]{2,1,0:T(8,128)(2,1)S(1)}, bf16[20,48,128]{2,1,0:T(8,128)(2,1)S(1)}, u32[]{:S(2)}, u32[]{:S(2)}) %collective-permute-start.2) | collective-permute-done | bytes 245792 | tf_op jit(solution)/shard_map/ppermute | solution.py:299
  40.3 1.3 %unpack.1 = bf16[1,48,5120]{2,1,0:T(8,128)(2,1)} custom-call(s32[40]{0:T(128)S(1)} %copy-done.5, bf16[20,48,128]{2,1,0:T(8,128)(2,1)S(1)} %collective-permute-done.1.refs_0_, bf16[20,48,128]{2,1,0:T(8,128)(2,1)S(1)} %collective-permute-done.2.refs_1_), custom_call_target="tpu_custom_call" | custom-call | bytes 983040 | tf_op jit(solution)/shard_map/unpack/pallas_call | solution.py:268
Async XLA Ops:
  0.0 1.0 %copy-start = (bf16[1,48,5120]{2,1,0:T(8,128)(2,1)S(1)}, bf16[1,48,5120]{2,1,0:T(8,128)(2,1)}, u32[]{:S(2)}) copy-start(bf16[1,48,5120]{2,1,0:T(8,128)(2,1)} %query_ref.3) | copy-start | bytes 1474564
  1.0 1.0 %copy-start.1 = (bf16[1,48,5120]{2,1,0:T(8,128)(2,1)S(1)}, bf16[1,48,5120]{2,1,0:T(8,128)(2,1)}, u32[]{:S(2)}) copy-start(bf16[1,48,5120]{2,1,0:T(8,128)(2,1)} %key_ref.3) | copy-start | bytes 1474564
  2.1 1.0 %copy-start.2 = (bf16[1,48,5120]{2,1,0:T(8,128)(2,1)S(1)}, bf16[1,48,5120]{2,1,0:T(8,128)(2,1)}, u32[]{:S(2)}) copy-start(bf16[1,48,5120]{2,1,0:T(8,128)(2,1)} %value_ref.3) | copy-start | bytes 1474564
  3.1 0.7 %copy-start.5 = (s32[40]{0:T(128)S(1)}, s32[40]{0:T(128)}, u32[]{:S(2)}) copy-start(s32[40]{0:T(128)} %order_ref.5) | copy-start | bytes 484
  3.7 20.5 %copy-start.3 = (bf16[1,20,192,128]{3,2,1,0:T(8,128)(2,1)S(1)}, bf16[1,20,192,128]{3,2,1,0:T(8,128)(2,1)}, u32[]{:S(2)}) copy-start(bf16[1,20,192,128]{3,2,1,0:T(8,128)(2,1)} %stale_key_ref.1) | copy-start | bytes 2949124
  3.8 20.5 %copy-start.4 = (bf16[1,20,192,128]{3,2,1,0:T(8,128)(2,1)S(1)}, bf16[1,20,192,128]{3,2,1,0:T(8,128)(2,1)}, u32[]{:S(2)}) copy-start(bf16[1,20,192,128]{3,2,1,0:T(8,128)(2,1)} %stale_value_ref.1) | copy-start | bytes 2949124
  4.7 19.5 %collective-permute-start = (bf16[3,20,48,128]{3,2,1,0:T(8,128)(2,1)S(1)}, bf16[3,20,48,128]{3,2,1,0:T(8,128)(2,1)S(1)}, u32[]{:S(2)}, u32[]{:S(2)}) collective-permute-start(bf16[3,20,48,128]{3,2,1,0:T(8,128)(2,1)S(1)} %pack.1), channel_id=1, source_target_pairs={{0,4},{4,0},{1,5},{5,1},{2,6},{6,2},{3,7},{7,3},{8,12},{12,8},{9,1... | collective-permute-start | bytes 2211848 | tf_op jit(solution)/shard_map/ppermute | solution.py:293
  30.8 5.7 %collective-permute-start.1 = (bf16[20,48,128]{2,1,0:T(8,128)(2,1)S(1)}, bf16[20,48,128]{2,1,0:T(8,128)(2,1)S(1)}, u32[]{:S(2)}, u32[]{:S(2)}) collective-permute-start(bf16[20,48,128]{2,1,0:T(8,128)(2,1)S(1)} %get-tuple-element.7), channel_id=1, source_target_pairs={{0,8},{8,16},{16,24},{24,0},{1,9},{9,17},{17,25},{25,1},{2,10},{10... | collective-permute-start | bytes 737288 | tf_op jit(solution)/shard_map/ppermute | solution.py:300
  30.8 9.5 %collective-permute-start.2 = (bf16[20,48,128]{2,1,0:T(8,128)(2,1)S(1)}, bf16[20,48,128]{2,1,0:T(8,128)(2,1)S(1)}, u32[]{:S(2)}, u32[]{:S(2)}) collective-permute-start(bf16[20,48,128]{2,1,0:T(8,128)(2,1)S(1)} %get-tuple-element.8), channel_id=1, source_target_pairs={{0,12},{4,8},{8,20},{12,16},{16,28},{20,24},{24,4},{28,0},{1,13},{... | collective-permute-start | bytes 737288 | tf_op jit(solution)/shard_map/ppermute | solution.py:299

commit v2 on v0

--- a/solution.py
+++ b/solution.py
@@ -1,9 +1,15 @@
+import functools
+
 import jax
 import jax.numpy as jnp
 from jax import lax
+from jax.experimental import pallas as pl
+from jax.experimental.pallas import tpu as pltpu
 from jax.sharding import PartitionSpec as P
 
 MICRO = 2
+EDGES = (0, 0.7, 1)
+KERNEL_VMEM = 8 << 20
 
 
 def from_behind(block, axis, distance):
@@ -44,7 +50,7 @@
     return count
 
 
-def per_device(query, key_new, value_new, stale_key, stale_value, head_order, tick):
+def wide_group(query, key_new, value_new, stale_key, stale_value, head_order, tick):
     group_size = lax.axis_size("seq")
     heads_dev = stale_key.shape[1]
     head_size = stale_key.shape[3]
@@ -64,14 +70,9 @@
 
     sent_query, sent_key, sent_value = (
         lax.all_to_all(
-            pack_heads(table, query, head_size), "seq", split_axis=1, concat_axis=0, tiled=True
-        ),
-        lax.all_to_all(
-            pack_heads(table, key_new, head_size), "seq", split_axis=1, concat_axis=0, tiled=True
-        ),
-        lax.all_to_all(
-            pack_heads(table, value_new, head_size), "seq", split_axis=1, concat_axis=0, tiled=True
-        ),
+            pack_heads(table, part, head_size), "seq", split_axis=1, concat_axis=0, tiled=True
+        )
+        for part in (query, key_new, value_new)
     )
     key_buf = with_fresh(stale_key, head_major(sent_key))
     value_buf = with_fresh(stale_value, head_major(sent_value))
@@ -107,6 +108,221 @@
     ).astype(jnp.bfloat16)
     result = merged.reshape(1, tok_rows, table.shape[2] * head_size)
     return from_behind(result, "segment", 1)
+
+
+def hbm_space():
+    return pl.BlockSpec(memory_space=pltpu.HBM)
+
+
+def in_hbm(array):
+    return pltpu.with_memory_space_constraint(array, pltpu.HBM)
+
+
+def vmem_space():
+    return pl.BlockSpec(memory_space=pltpu.VMEM)
+
+
+def scalar_space():
+    return pl.BlockSpec(memory_space=pltpu.SMEM)
+
+
+def columns_of(order_ref, unit, head_size):
+    return pl.ds(pl.multiple_of(order_ref[unit] * head_size, head_size), head_size)
+
+
+def moved(count):
+    return pl.CostEstimate(flops=0, bytes_accessed=2 * count, transcendentals=0)
+
+
+def pack_body(bounds, given_ref, query_ref, key_ref, value_ref, order_ref, own_ref, *refs):
+    send_refs, (buf, sems) = refs[: len(bounds)], refs[len(bounds) :]
+    me = lax.axis_index("seq")
+    head_size = own_ref.shape[3]
+    copies = [
+        pltpu.make_async_copy(source.at[0], buf.at[place], sems.at[place])
+        for place, source in enumerate((key_ref, value_ref, query_ref))
+    ] + [pltpu.make_async_copy(given_ref, order_ref, sems.at[3])]
+    for copy in copies:
+        copy.start()
+    for copy in copies:
+        copy.wait()
+    for (low, heads), send_ref in zip(bounds, send_refs):
+        for l in range(heads):
+            columns = columns_of(order_ref, 2 * (low + l) + 1 - me, head_size)
+            for place in range(3):
+                send_ref[place, l] = buf[place, :, columns]
+    for l in range(own_ref.shape[1]):
+        columns = columns_of(order_ref, 2 * l + me, head_size)
+        for place in range(3):
+            own_ref[place, l] = buf[place, :, columns]
+
+
+def pack(bounds, head_order, query, key_new, value_new):
+    tok_rows, width = query.shape[1:]
+    head_size = width // head_order.shape[0]
+    own = sum(heads for _, heads in bounds)
+    shapes = [pltpu.SMEM(head_order.shape, head_order.dtype)] + [
+        jax.ShapeDtypeStruct((3, heads, tok_rows, head_size), query.dtype)
+        for heads in [own] + [heads for _, heads in bounds]
+    ]
+    order, own, *sends = pl.pallas_call(
+        functools.partial(pack_body, bounds),
+        out_shape=shapes,
+        in_specs=[hbm_space()] * 4,
+        out_specs=[scalar_space()] + [vmem_space()] * (len(shapes) - 1),
+        scratch_shapes=[
+            pltpu.VMEM((3, tok_rows, width), query.dtype),
+            pltpu.SemaphoreType.DMA((4,)),
+        ],
+        cost_estimate=moved(6 * tok_rows * width),
+        compiler_params=pltpu.CompilerParams(vmem_limit_bytes=KERNEL_VMEM),
+        name="pack",
+    )(*(in_hbm(x) for x in (head_order, query, key_new, value_new)))
+    return order, own, sends
+
+
+def keep_body(tick_ref, stale_key_ref, stale_value_ref, key_ref, value_ref, sems):
+    patch_tok = key_ref.shape[1]
+    kept = (tick_ref[0] - lax.axis_index("segment") + 1) & 1
+    rows = pl.ds(pl.multiple_of(kept * patch_tok, patch_tok), patch_tok)
+    copies = [
+        pltpu.make_async_copy(source.at[0, :, rows], target, sems.at[i])
+        for i, (source, target) in enumerate(
+            ((stale_key_ref, key_ref), (stale_value_ref, value_ref))
+        )
+    ]
+    for copy in copies:
+        copy.start()
+    for copy in copies:
+        copy.wait()
+
+
+def keep(tick, stale_key, stale_value):
+    _, heads, length, head_size = stale_key.shape
+    kept = jax.ShapeDtypeStruct((heads, length // MICRO, head_size), stale_key.dtype)
+    return pl.pallas_call(
+        keep_body,
+        out_shape=(kept, kept),
+        in_specs=[scalar_space()] + [hbm_space()] * 2,
+        out_specs=(vmem_space(),) * 2,
+        scratch_shapes=[pltpu.SemaphoreType.DMA((2,))],
+        cost_estimate=moved(2 * heads * length * head_size),
+        compiler_params=pltpu.CompilerParams(vmem_limit_bytes=KERNEL_VMEM),
+        name="keep",
+    )(tick, in_hbm(stale_key), in_hbm(stale_value))
+
+
+def attend_body(low, recv_ref, own_ref, kept_key_ref, kept_value_ref, near_ref, far_ref):
+    heads, tok_rows, head_size = near_ref.shape
+    factor = head_size ** (-0.5) * 1.4426950408889634
+    ones = jnp.ones((2 * kept_key_ref.shape[1], head_size), near_ref.dtype)
+    for l in range(heads):
+        at = low + l
+        keys = jnp.concatenate([kept_key_ref[at], own_ref[0, at], recv_ref[0, l]], axis=0)
+        values = jnp.concatenate([kept_value_ref[at], own_ref[1, at], recv_ref[1, l]], axis=0)
+        queries = jnp.concatenate([own_ref[2, at], recv_ref[2, l]], axis=0)
+        scores = lax.dot_general(
+            keys, queries, (((1,), (1,)), ((), ())), preferred_element_type=jnp.float32
+        )
+        top = jnp.max(scores, axis=0, keepdims=True)
+        weights = jnp.exp2((scores - top) * factor).astype(near_ref.dtype)
+        both = lax.dot_general(
+            weights,
+            jnp.concatenate([values, ones], axis=1),
+            (((0,), (0,)), ((), ())),
+            preferred_element_type=jnp.float32,
+        )
+        result = (both[:, :head_size] / both[:, head_size:]).astype(near_ref.dtype)
+        near_ref[l] = result[:tok_rows]
+        far_ref[l] = result[tok_rows:]
+
+
+def attend(low, heads, received, own, kept_key, kept_value):
+    tok_rows, head_size = own.shape[2:]
+    patch_tok = 2 * tok_rows
+    length = MICRO * patch_tok
+    out = jax.ShapeDtypeStruct((heads, tok_rows, head_size), own.dtype)
+    return pl.pallas_call(
+        functools.partial(attend_body, low),
+        out_shape=(out, out),
+        in_specs=[vmem_space()] * 4,
+        out_specs=(vmem_space(),) * 2,
+        cost_estimate=pl.CostEstimate(
+            flops=6 * heads * patch_tok * length * head_size,
+            bytes_accessed=2 * heads * head_size * (2 * length + 2 * patch_tok),
+            transcendentals=heads * patch_tok * length,
+        ),
+        compiler_params=pltpu.CompilerParams(vmem_limit_bytes=KERNEL_VMEM),
+        name="attend",
+    )(received, own, kept_key, kept_value)
+
+
+def unpack_body(bounds, order_ref, *refs):
+    count = len(bounds)
+    near, far = refs[:count], refs[count : 2 * count]
+    out_ref, sem = refs[2 * count :]
+    me = lax.axis_index("seq")
+    head_size = near[0].shape[2]
+    for c, (low, heads) in enumerate(bounds):
+        for l in range(heads):
+            for side, source in ((me, near[c]), (1 - me, far[c])):
+                columns = columns_of(order_ref, 2 * (low + l) + side, head_size)
+                pltpu.make_async_copy(source.at[l], out_ref.at[0, :, columns], sem).start()
+    pltpu.make_async_copy(out_ref, out_ref, sem).wait()
+
+
+def unpack(bounds, head_order, near, far):
+    tok_rows, head_size = near[0].shape[1:]
+    shape = (1, tok_rows, head_order.shape[0] * head_size)
+    return pl.pallas_call(
+        functools.partial(unpack_body, bounds),
+        out_shape=jax.ShapeDtypeStruct(shape, near[0].dtype),
+        in_specs=[scalar_space()] + [vmem_space()] * (2 * len(bounds)),
+        out_specs=hbm_space(),
+        scratch_shapes=[pltpu.SemaphoreType.DMA],
+        cost_estimate=moved(2 * shape[1] * shape[2]),
+        compiler_params=pltpu.CompilerParams(vmem_limit_bytes=KERNEL_VMEM),
+        name="unpack",
+    )(head_order, *near, *far)
+
+
+def chunks(heads_dev):
+    edges = [round(heads_dev * edge) for edge in EDGES]
+    return [(a, b - a) for a, b in zip(edges[:-1], edges[1:])]
+
+
+def pair_group(query, key_new, value_new, stale_key, stale_value, head_order, tick):
+    segments = lax.axis_size("segment")
+    bounds = chunks(stale_key.shape[1])
+    ahead = [(s, (s + 1) % segments) for s in range(segments)]
+    across = [(2 * s + j, 2 * t + 1 - j) for s, t in ahead for j in range(2)]
+
+    order, own, sends = pack(bounds, head_order, query, key_new, value_new)
+    received = [lax.ppermute(send, "seq", [(0, 1), (1, 0)]) for send in sends]
+    kept_key, kept_value = keep(tick, stale_key, stale_value)
+    near, far = [], []
+    for (low, heads), got in zip(bounds, received):
+        if far:
+            got, _ = lax.optimization_barrier((got, theirs))
+        ours, theirs = attend(low, heads, got, own, kept_key, kept_value)
+        far.append(lax.ppermute(theirs, ("segment", "seq"), across))
+        near.append(lax.ppermute(ours, "segment", ahead))
+    return unpack(bounds, order, near, far)
+
+
+def per_device(query, key_new, value_new, stale_key, stale_value, head_order, tick):
+    group_size = lax.axis_size("seq")
+    heads = head_order.shape[0]
+    tok_rows, head_size = query.shape[1], stale_key.shape[3]
+    paired = (
+        group_size == 2
+        and heads == 2 * stale_key.shape[1]
+        and stale_key.shape[2] == MICRO * 2 * tok_rows
+        and tok_rows % 16 == 0
+        and head_size % 128 == 0
+    )
+    chosen = pair_group if paired else wide_group
+    return chosen(query, key_new, value_new, stale_key, stale_value, head_order, tick)
 
 
 def solution(mesh):

time: 70 us -> 28.7 us (0.41)
  waiting for transfers between devices: 25.4 us -> 13.5 us
  matrix products: 11.4 us -> 0 us
  blocking collectives: 9.35 us -> 0 us
  local copies, waits for them, and re-layouts: 6.24 us -> 0 us
  Pallas kernels: 0 us -> 5.01 us
  other arithmetic: 4.44 us -> 0 us
  starting transfers between devices: 11.3 us -> 9.24 us
    all_to_all x3 -> x0, waiting for transfers between devices: 17.2 us -> none  [the longest x1 7 us: per_device(): lax.all_to_all(pack_heads(table, key_new, head_size), 'seq', split_axis=1...]
    dot_general x44 -> x0, matrix products: 11.4 us -> none  [the longest x20 5.46 us: one_block(): jnp.dot(query_rows, key_rows.T, preferred_element_type=jnp.float32)]
    all_to_all x3 -> x0, starting transfers between devices: 11.2 us -> none  [the longest x1 4.23 us: per_device(): lax.all_to_all(pack_heads(table, key_new, head_size), 'seq', split_axis=1...]
    all_to_all x1 -> x0, blocking collectives: 9.35 us -> none  [per_device(): lax.all_to_all(outgoing, 'seq', split_axis=0, concat_axis=1, tiled=True)]
    ppermute x1 -> x6, starting transfers between devices: 0.06 us -> 9.24 us  [the longest x2 3.15 us: pair_group(): near.append(lax.ppermute(ours, 'segment', ahead))]
    ppermute x1 -> x6, waiting for transfers between devices: 8.24 us -> 13.5 us  [the longest x2 10.6 us: pair_group(): received = [lax.ppermute(send, 'seq', [(0, 1), (1, 0)]) for send in sends]]
    pallas_call x0 -> x5, Pallas kernels: none -> 5.01 us  [the longest x1 1.75 us: pack(): pl.pallas_call(functools.partial(pack_body, bounds), out_shape=shapes, in...]
    reduce_sum x21 -> x0, other arithmetic: 4.29 us -> none  [the longest x20 3.81 us: one_block(): total = jnp.sum(weights, axis=-1, keepdims=True, dtype=jnp.float32)]
  transfers between devices with their start and end apart: 4 -> 6, of which waited for: 4 -> 3; matrix products, arithmetic and copies ran while one was open for 4% -> 0% of each run, Pallas kernels for 0% -> 9%
where the time goes in v2:
time: 28.7 us; the launch traced here: 28.5 us
  waiting for transfers between devices  13.5 us (47%)
  starting transfers between devices  9.24 us (32%)
  Pallas kernels  5.01 us (17%)
  between operations  0.7 us (2%)
    ppermute x2, waiting for transfers between devices, pair_group(): received = [lax.ppermute(send, 'seq', [(0, 1), (1, 0)]) for send in sends]  10.6 us
    ppermute x2, starting transfers between devices, pair_group(): near.append(lax.ppermute(ours, 'segment', ahead))  3.15 us
    ppermute x2, starting transfers between devices, pair_group(): received = [lax.ppermute(send, 'seq', [(0, 1), (1, 0)]) for send in sends]  3.11 us
    ppermute x2, starting transfers between devices, pair_group(): far.append(lax.ppermute(theirs, ('segment', 'seq'), across))  2.98 us
    ppermute x2, waiting for transfers between devices, pair_group(): near.append(lax.ppermute(ours, 'segment', ahead))  2.37 us
    pallas_call x1, Pallas kernels, pack(): pl.pallas_call(functools.partial(pack_body, bounds), out_shape=shapes, in...  1.75 us
    pallas_call x2, Pallas kernels, attend(): pl.pallas_call(functools.partial(attend_body, low), out_shape=(out, out),...  1.3 us
    pallas_call x1, Pallas kernels, keep(): pl.pallas_call(keep_body, out_shape=(kept, kept), in_specs=[scalar_space(...  1.21 us
  transfers between devices with their start and end apart: 6, of which 3 were waited for; matrix products, arithmetic and copies ran while one was open for 0% of the time, Pallas kernels for 9%

profile of v2, /device:TPU:0, one launch (start us, length us, event | category | flops | bytes accessed | tf_op | source)
XLA Modules:
  0.0 28.5 jit_solution(1413628964025140814)
XLA Ops:
  0.0 1.8 %pack.1 = (s32[40]{0:T(128)S(4)}, bf16[3,20,48,128]{3,2,1,0:T(8,128)(2,1)S(1)}, bf16[3,14,48,128]{3,2,1,0:T(8,128)(2,1)S(1)}, bf16[3,6,48,128]{3,2,1,0:T(8,128)(2,1)S(1)}) custom-call(s32[40]{0:T(128)} %given_ref.1, bf16[1,48,5120]{2,1,0:T(8,128)(2,1)} %query_ref.1, bf16[1,48,5120]{2,1,0:T(8,128)(2,1)} %key_ref.1, bf16[1,48,5120]{2,1,0:T(8,128)(2,1)} %value_ref.1), custom_call_target="tpu_custom_call" | custom-call | bytes 2949120 | tf_op jit(solution)/shard_map/pack/pallas_call | solution.py:168
  1.8 3.0 %collective-permute-start = (bf16[3,14,48,128]{3,2,1,0:T(8,128)(2,1)S(1)}, bf16[3,14,48,128]{3,2,1,0:T(8,128)(2,1)S(1)}, u32[]{:S(2)}, u32[]{:S(2)}) collective-permute-start(bf16[3,14,48,128]{3,2,1,0:T(8,128)(2,1)S(1)} %get-tuple-element.17), channel_id=1, source_target_pairs={{0,4},{4,0},{1,5},{5,1},{2,6},{6,2},{3,7},{7,3},{8,12},{12,8},{9,1... | collective-permute-start | bytes 1548296 | tf_op jit(solution)/shard_map/ppermute | solution.py:301
  4.8 0.1 collective-permute-start.2
  5.5 1.2 %keep.1 = (bf16[20,96,128]{2,1,0:T(8,128)(2,1)S(1)}, bf16[20,96,128]{2,1,0:T(8,128)(2,1)S(1)}) custom-call(s32[1]{0:T(128)S(6)} %copy.8.tick_ref, bf16[1,20,192,128]{3,2,1,0:T(8,128)(2,1)} %stale_key_ref.1, bf16[1,20,192,128]{3,2,1,0:T(8,128)(2,1)} %stale_value_ref.1), custom_call_target="tpu_custom_call" | custom-call | bytes 1966080 | tf_op jit(solution)/shard_map/keep/pallas_call | solution.py:203
  6.7 10.6 %collective-permute-done.recv_ref = bf16[3,14,48,128]{3,2,1,0:T(8,128)(2,1)S(1)} collective-permute-done((bf16[3,14,48,128]{3,2,1,0:T(8,128)(2,1)S(1)}, bf16[3,14,48,128]{3,2,1,0:T(8,128)(2,1)S(1)}, u32[]{:S(2)}, u32[]{:S(2)}) %collective-permute-start) | collective-permute-done | bytes 516128 | tf_op jit(solution)/shard_map/ppermute | solution.py:301
  17.4 0.8 %attend.2 = (bf16[14,48,128]{2,1,0:T(8,128)(2,1)S(1)}, bf16[14,48,128]{2,1,0:T(8,128)(2,1)S(1)}) custom-call(bf16[3,14,48,128]{3,2,1,0:T(8,128)(2,1)S(1)} %collective-permute-done.recv_ref, bf16[3,20,48,128]{3,2,1,0:T(8,128)(2,1)S(1)} %get-tuple-element.18.own_ref, bf16[20,96,128]{2,1,0:T(8,128)(2,1)S(1)} %get-tuple-element.19.kept_key_ref, ...), custom_call_target="tpu_custom_call" | custom-call | flops 198180864 | bytes 2064384 | tf_op jit(solution)/shard_map/attend/pallas_call | solution.py:245
  18.1 0.1 collective-permute-start.4
  18.2 3.1 %collective-permute-start.1 = (bf16[14,48,128]{2,1,0:T(8,128)(2,1)S(1)}, bf16[14,48,128]{2,1,0:T(8,128)(2,1)S(1)}, u32[]{:S(2)}, u32[]{:S(2)}) collective-permute-start(bf16[14,48,128]{2,1,0:T(8,128)(2,1)S(1)} %get-tuple-element.21), channel_id=1, source_target_pairs={{0,8},{8,16},{16,24},{24,0},{1,9},{9,17},{17,25},{25,1},{2,10},{10... | collective-permute-start | bytes 516104 | tf_op jit(solution)/shard_map/ppermute | solution.py:309
  21.3 0.0 collective-permute-done.2.recv_ref
  21.3 0.5 %attend.3 = (bf16[6,48,128]{2,1,0:T(8,128)(2,1)S(1)}, bf16[6,48,128]{2,1,0:T(8,128)(2,1)S(1)}) custom-call(bf16[3,6,48,128]{3,2,1,0:T(8,128)(2,1)S(1)} %collective-permute-done.2.recv_ref, bf16[3,20,48,128]{3,2,1,0:T(8,128)(2,1)S(1)} %get-tuple-element.18.own_ref, bf16[20,96,128]{2,1,0:T(8,128)(2,1)S(1)} %get-tuple-element.19.kept_key_ref, ...), custom_call_target="tpu_custom_call" | custom-call | flops 84934656 | bytes 884736 | tf_op jit(solution)/shard_map/attend/pallas_call | solution.py:245
  21.8 0.1 collective-permute-start.3
  21.9 2.9 %collective-permute-start.5 = (bf16[6,48,128]{2,1,0:T(8,128)(2,1)S(1)}, bf16[6,48,128]{2,1,0:T(8,128)(2,1)S(1)}, u32[]{:S(2)}, u32[]{:S(2)}) collective-permute-start(bf16[6,48,128]{2,1,0:T(8,128)(2,1)S(1)} %get-tuple-element.26), channel_id=1, source_target_pairs={{0,12},{4,8},{8,20},{12,16},{16,28},{20,24},{24,4},{28,0},{1,13},{... | collective-permute-start | bytes 221192 | tf_op jit(solution)/shard_map/ppermute | solution.py:308
  24.8 2.4 %collective-permute-done.3.refs_1_ = bf16[6,48,128]{2,1,0:T(8,128)(2,1)S(1)} collective-permute-done((bf16[6,48,128]{2,1,0:T(8,128)(2,1)S(1)}, bf16[6,48,128]{2,1,0:T(8,128)(2,1)S(1)}, u32[]{:S(2)}, u32[]{:S(2)}) %collective-permute-start.3) | collective-permute-done | bytes 73760 | tf_op jit(solution)/shard_map/ppermute | solution.py:309
  27.2 0.5 %collective-permute-done.5.refs_3_ = bf16[6,48,128]{2,1,0:T(8,128)(2,1)S(1)} collective-permute-done((bf16[6,48,128]{2,1,0:T(8,128)(2,1)S(1)}, bf16[6,48,128]{2,1,0:T(8,128)(2,1)S(1)}, u32[]{:S(2)}, u32[]{:S(2)}) %collective-permute-start.5) | collective-permute-done | bytes 73760 | tf_op jit(solution)/shard_map/ppermute | solution.py:308
  27.7 0.0 collective-permute-done.4.refs_2_
  27.7 0.0 collective-permute-done.1.refs_0_
  27.7 0.8 %unpack.1 = bf16[1,48,5120]{2,1,0:T(8,128)(2,1)} custom-call(s32[40]{0:T(128)S(4)} %get-tuple-element.16.order_ref, bf16[14,48,128]{2,1,0:T(8,128)(2,1)S(1)} %collective-permute-done.1.refs_0_, bf16[6,48,128]{2,1,0:T(8,128)(2,1)S(1)} %collective-permute-done.3.refs_1_, bf16[14,48,128]{2,1,0:T(8,128)(2,1)S(1)} %collective-permute-done.4.refs_2_, ...), custom_call_target="tpu_custom_call" | custom-call | bytes 983040 | tf_op jit(solution)/shard_map/unpack/pallas_call | solution.py:277
Async XLA Ops:
  1.8 15.6 %collective-permute-start = (bf16[3,14,48,128]{3,2,1,0:T(8,128)(2,1)S(1)}, bf16[3,14,48,128]{3,2,1,0:T(8,128)(2,1)S(1)}, u32[]{:S(2)}, u32[]{:S(2)}) collective-permute-start(bf16[3,14,48,128]{3,2,1,0:T(8,128)(2,1)S(1)} %get-tuple-element.17), channel_id=1, source_target_pairs={{0,4},{4,0},{1,5},{5,1},{2,6},{6,2},{3,7},{7,3},{8,12},{12,8},{9,1... | collective-permute-start | bytes 1548296 | tf_op jit(solution)/shard_map/ppermute | solution.py:301
  4.8 16.5 %collective-permute-start.2 = (bf16[3,6,48,128]{3,2,1,0:T(8,128)(2,1)S(1)}, bf16[3,6,48,128]{3,2,1,0:T(8,128)(2,1)S(1)}, u32[]{:S(2)}, u32[]{:S(2)}) collective-permute-start(bf16[3,6,48,128]{3,2,1,0:T(8,128)(2,1)S(1)} %get-tuple-element.22), channel_id=1, source_target_pairs={{0,4},{4,0},{1,5},{5,1},{2,6},{6,2},{3,7},{7,3},{8,12},{12,8},{9,1... | collective-permute-start | bytes 663560 | tf_op jit(solution)/shard_map/ppermute | solution.py:301
  18.1 9.6 %collective-permute-start.4 = (bf16[14,48,128]{2,1,0:T(8,128)(2,1)S(1)}, bf16[14,48,128]{2,1,0:T(8,128)(2,1)S(1)}, u32[]{:S(2)}, u32[]{:S(2)}) collective-permute-start(bf16[14,48,128]{2,1,0:T(8,128)(2,1)S(1)} %get-tuple-element.23), channel_id=1, source_target_pairs={{0,12},{4,8},{8,20},{12,16},{16,28},{20,24},{24,4},{28,0},{1,13},{... | collective-permute-start | bytes 516104 | tf_op jit(solution)/shard_map/ppermute | solution.py:308
  18.2 9.5 %collective-permute-start.1 = (bf16[14,48,128]{2,1,0:T(8,128)(2,1)S(1)}, bf16[14,48,128]{2,1,0:T(8,128)(2,1)S(1)}, u32[]{:S(2)}, u32[]{:S(2)}) collective-permute-start(bf16[14,48,128]{2,1,0:T(8,128)(2,1)S(1)} %get-tuple-element.21), channel_id=1, source_target_pairs={{0,8},{8,16},{16,24},{24,0},{1,9},{9,17},{17,25},{25,1},{2,10},{10... | collective-permute-start | bytes 516104 | tf_op jit(solution)/shard_map/ppermute | solution.py:309
  21.8 5.4 %collective-permute-start.3 = (bf16[6,48,128]{2,1,0:T(8,128)(2,1)S(1)}, bf16[6,48,128]{2,1,0:T(8,128)(2,1)S(1)}, u32[]{:S(2)}, u32[]{:S(2)}) collective-permute-start(bf16[6,48,128]{2,1,0:T(8,128)(2,1)S(1)} %get-tuple-element.25), channel_id=1, source_target_pairs={{0,8},{8,16},{16,24},{24,0},{1,9},{9,17},{17,25},{25,1},{2,10},{10... | collective-permute-start | bytes 221192 | tf_op jit(solution)/shard_map/ppermute | solution.py:309
  21.9 5.8 %collective-permute-start.5 = (bf16[6,48,128]{2,1,0:T(8,128)(2,1)S(1)}, bf16[6,48,128]{2,1,0:T(8,128)(2,1)S(1)}, u32[]{:S(2)}, u32[]{:S(2)}) collective-permute-start(bf16[6,48,128]{2,1,0:T(8,128)(2,1)S(1)} %get-tuple-element.26), channel_id=1, source_target_pairs={{0,12},{4,8},{8,20},{12,16},{16,28},{20,24},{24,4},{28,0},{1,13},{... | collective-permute-start | bytes 221192 | tf_op jit(solution)/shard_map/ppermute | solution.py:308

commit v3 on v2

--- a/solution.py
+++ b/solution.py
@@ -134,55 +134,61 @@
     return pl.CostEstimate(flops=0, bytes_accessed=2 * count, transcendentals=0)
 
 
-def pack_body(bounds, given_ref, query_ref, key_ref, value_ref, order_ref, own_ref, *refs):
-    send_refs, (buf, sems) = refs[: len(bounds)], refs[len(bounds) :]
-    me = lax.axis_index("seq")
-    head_size = own_ref.shape[3]
+def pack_body(bounds, given_ref, query_ref, key_ref, value_ref, order_ref, fresh_ref, *refs):
+    send_refs, (sems,) = refs[: len(bounds)], refs[len(bounds) :]
+    other = 1 - lax.axis_index("seq")
+    head_size = send_refs[0].shape[3]
     copies = [
-        pltpu.make_async_copy(source.at[0], buf.at[place], sems.at[place])
+        pltpu.make_async_copy(source.at[0], fresh_ref.at[place], sems.at[place])
         for place, source in enumerate((key_ref, value_ref, query_ref))
     ] + [pltpu.make_async_copy(given_ref, order_ref, sems.at[3])]
     for copy in copies:
         copy.start()
-    for copy in copies:
-        copy.wait()
-    for (low, heads), send_ref in zip(bounds, send_refs):
-        for l in range(heads):
-            columns = columns_of(order_ref, 2 * (low + l) + 1 - me, head_size)
-            for place in range(3):
-                send_ref[place, l] = buf[place, :, columns]
-    for l in range(own_ref.shape[1]):
-        columns = columns_of(order_ref, 2 * l + me, head_size)
-        for place in range(3):
-            own_ref[place, l] = buf[place, :, columns]
+    copies[3].wait()
+    for place in range(3):
+        copies[place].wait()
+        for (low, heads), send_ref in zip(bounds, send_refs):
+            for l in range(heads):
+                columns = columns_of(order_ref, 2 * (low + l) + other, head_size)
+                send_ref[place, l] = fresh_ref[place, :, columns]
 
 
 def pack(bounds, head_order, query, key_new, value_new):
     tok_rows, width = query.shape[1:]
     head_size = width // head_order.shape[0]
-    own = sum(heads for _, heads in bounds)
-    shapes = [pltpu.SMEM(head_order.shape, head_order.dtype)] + [
-        jax.ShapeDtypeStruct((3, heads, tok_rows, head_size), query.dtype)
-        for heads in [own] + [heads for _, heads in bounds]
+    shapes = [
+        pltpu.SMEM(head_order.shape, head_order.dtype),
+        jax.ShapeDtypeStruct((3, tok_rows, width), query.dtype),
+    ] + [
+        jax.ShapeDtypeStruct((3, heads, tok_rows, head_size), query.dtype) for _, heads in bounds
     ]
-    order, own, *sends = pl.pallas_call(
+    order, fresh, *sends = pl.pallas_call(
         functools.partial(pack_body, bounds),
         out_shape=shapes,
         in_specs=[hbm_space()] * 4,
         out_specs=[scalar_space()] + [vmem_space()] * (len(shapes) - 1),
-        scratch_shapes=[
-            pltpu.VMEM((3, tok_rows, width), query.dtype),
-            pltpu.SemaphoreType.DMA((4,)),
-        ],
+        scratch_shapes=[pltpu.SemaphoreType.DMA((4,))],
         cost_estimate=moved(6 * tok_rows * width),
         compiler_params=pltpu.CompilerParams(vmem_limit_bytes=KERNEL_VMEM),
         name="pack",
     )(*(in_hbm(x) for x in (head_order, query, key_new, value_new)))
-    return order, own, sends
-
-
-def keep_body(tick_ref, stale_key_ref, stale_value_ref, key_ref, value_ref, sems):
+    return order, fresh, sends
+
+
+def keep_body(
+    order_ref,
+    tick_ref,
+    fresh_ref,
+    stale_key_ref,
+    stale_value_ref,
+    own_ref,
+    key_ref,
+    value_ref,
+    sems,
+):
+    me = lax.axis_index("seq")
     patch_tok = key_ref.shape[1]
+    head_size = own_ref.shape[3]
     kept = (tick_ref[0] - lax.axis_index("segment") + 1) & 1
     rows = pl.ds(pl.multiple_of(kept * patch_tok, patch_tok), patch_tok)
     copies = [
@@ -193,29 +199,35 @@
     ]
     for copy in copies:
         copy.start()
+    for l in range(own_ref.shape[1]):
+        columns = columns_of(order_ref, 2 * l + me, head_size)
+        for place in range(3):
+            own_ref[place, l] = fresh_ref[place, :, columns]
     for copy in copies:
         copy.wait()
 
 
-def keep(tick, stale_key, stale_value):
+def keep(order, fresh, tick, stale_key, stale_value):
     _, heads, length, head_size = stale_key.shape
+    own = jax.ShapeDtypeStruct((3, heads, fresh.shape[1], head_size), fresh.dtype)
     kept = jax.ShapeDtypeStruct((heads, length // MICRO, head_size), stale_key.dtype)
     return pl.pallas_call(
         keep_body,
-        out_shape=(kept, kept),
-        in_specs=[scalar_space()] + [hbm_space()] * 2,
-        out_specs=(vmem_space(),) * 2,
+        out_shape=(own, kept, kept),
+        in_specs=[scalar_space()] * 2 + [vmem_space()] + [hbm_space()] * 2,
+        out_specs=(vmem_space(),) * 3,
         scratch_shapes=[pltpu.SemaphoreType.DMA((2,))],
         cost_estimate=moved(2 * heads * length * head_size),
         compiler_params=pltpu.CompilerParams(vmem_limit_bytes=KERNEL_VMEM),
         name="keep",
-    )(tick, in_hbm(stale_key), in_hbm(stale_value))
-
-
-def attend_body(low, recv_ref, own_ref, kept_key_ref, kept_value_ref, near_ref, far_ref):
-    heads, tok_rows, head_size = near_ref.shape
+    )(order, tick, fresh, in_hbm(stale_key), in_hbm(stale_value))
+
+
+def attend_body(low, recv_ref, own_ref, kept_key_ref, kept_value_ref, first_ref, second_ref):
+    odd = (lax.axis_index("segment") & 1) == 1
+    heads, tok_rows, head_size = first_ref.shape
     factor = head_size ** (-0.5) * 1.4426950408889634
-    ones = jnp.ones((2 * kept_key_ref.shape[1], head_size), near_ref.dtype)
+    ones = jnp.ones((2 * kept_key_ref.shape[1], head_size), first_ref.dtype)
     for l in range(heads):
         at = low + l
         keys = jnp.concatenate([kept_key_ref[at], own_ref[0, at], recv_ref[0, l]], axis=0)
@@ -225,16 +237,16 @@
             keys, queries, (((1,), (1,)), ((), ())), preferred_element_type=jnp.float32
         )
         top = jnp.max(scores, axis=0, keepdims=True)
-        weights = jnp.exp2((scores - top) * factor).astype(near_ref.dtype)
+        weights = jnp.exp2((scores - top) * factor).astype(first_ref.dtype)
         both = lax.dot_general(
             weights,
             jnp.concatenate([values, ones], axis=1),
             (((0,), (0,)), ((), ())),
             preferred_element_type=jnp.float32,
         )
-        result = (both[:, :head_size] / both[:, head_size:]).astype(near_ref.dtype)
-        near_ref[l] = result[:tok_rows]
-        far_ref[l] = result[tok_rows:]
+        result = (both[:, :head_size] / both[:, head_size:]).astype(first_ref.dtype)
+        first_ref[l] = jnp.where(odd, result[tok_rows:], result[:tok_rows])
+        second_ref[l] = jnp.where(odd, result[:tok_rows], result[tok_rows:])
 
 
 def attend(low, heads, received, own, kept_key, kept_value):
@@ -257,33 +269,32 @@
     )(received, own, kept_key, kept_value)
 
 
-def unpack_body(bounds, order_ref, *refs):
-    count = len(bounds)
-    near, far = refs[:count], refs[count : 2 * count]
-    out_ref, sem = refs[2 * count :]
-    me = lax.axis_index("seq")
-    head_size = near[0].shape[2]
-    for c, (low, heads) in enumerate(bounds):
-        for l in range(heads):
-            for side, source in ((me, near[c]), (1 - me, far[c])):
-                columns = columns_of(order_ref, 2 * (low + l) + side, head_size)
-                pltpu.make_async_copy(source.at[l], out_ref.at[0, :, columns], sem).start()
-    pltpu.make_async_copy(out_ref, out_ref, sem).wait()
-
-
-def unpack(bounds, head_order, near, far):
-    tok_rows, head_size = near[0].shape[1:]
-    shape = (1, tok_rows, head_order.shape[0] * head_size)
+def unpack_body(low, order_ref, first_ref, second_ref, *refs):
+    out_ref, sems = refs[-2:]
+    side = lax.axis_index("seq") ^ ((lax.axis_index("segment") + 1) & 1)
+    heads, _, head_size = first_ref.shape
+    for l in range(heads):
+        for i, (owner, piece) in enumerate(((side, first_ref), (1 - side, second_ref))):
+            columns = columns_of(order_ref, 2 * (low + l) + owner, head_size)
+            pltpu.make_async_copy(piece.at[l], out_ref.at[0, :, columns], sems.at[i]).start()
+    for i, piece in enumerate((first_ref, second_ref)):
+        pltpu.make_async_copy(piece, piece, sems.at[i]).wait()
+
+
+def unpack(low, order, first, second, out):
+    heads, tok_rows, head_size = first.shape
+    shape = (1, tok_rows, order.shape[0] * head_size)
     return pl.pallas_call(
-        functools.partial(unpack_body, bounds),
-        out_shape=jax.ShapeDtypeStruct(shape, near[0].dtype),
-        in_specs=[scalar_space()] + [vmem_space()] * (2 * len(bounds)),
+        functools.partial(unpack_body, low),
+        out_shape=pltpu.HBM(shape, first.dtype),
+        in_specs=[scalar_space()] + [vmem_space()] * 2 + [hbm_space()] * (out is not None),
         out_specs=hbm_space(),
-        scratch_shapes=[pltpu.SemaphoreType.DMA],
-        cost_estimate=moved(2 * shape[1] * shape[2]),
+        input_output_aliases={} if out is None else {3: 0},
+        scratch_shapes=[pltpu.SemaphoreType.DMA((2,))],
+        cost_estimate=moved(4 * heads * tok_rows * head_size),
         compiler_params=pltpu.CompilerParams(vmem_limit_bytes=KERNEL_VMEM),
         name="unpack",
-    )(head_order, *near, *far)
+    )(order, first, second, *(() if out is None else (out,)))
 
 
 def chunks(heads_dev):
@@ -294,20 +305,29 @@
 def pair_group(query, key_new, value_new, stale_key, stale_value, head_order, tick):
     segments = lax.axis_size("segment")
     bounds = chunks(stale_key.shape[1])
-    ahead = [(s, (s + 1) % segments) for s in range(segments)]
-    across = [(2 * s + j, 2 * t + 1 - j) for s, t in ahead for j in range(2)]
-
-    order, own, sends = pack(bounds, head_order, query, key_new, value_new)
+
+    def handed(block, crossed):
+        route = [
+            (2 * s + j, 2 * ((s + 1) % segments) + (1 - j if s % 2 == crossed else j))
+            for s in range(segments)
+            for j in range(2)
+        ]
+        return lax.ppermute(block, ("segment", "seq"), route)
+
+    order, fresh, sends = pack(bounds, head_order, query, key_new, value_new)
     received = [lax.ppermute(send, "seq", [(0, 1), (1, 0)]) for send in sends]
-    kept_key, kept_value = keep(tick, stale_key, stale_value)
-    near, far = [], []
+    own, kept_key, kept_value = keep(order, fresh, tick, stale_key, stale_value)
+    results, last = [], None
     for (low, heads), got in zip(bounds, received):
-        if far:
-            got, _ = lax.optimization_barrier((got, theirs))
-        ours, theirs = attend(low, heads, got, own, kept_key, kept_value)
-        far.append(lax.ppermute(theirs, ("segment", "seq"), across))
-        near.append(lax.ppermute(ours, "segment", ahead))
-    return unpack(bounds, order, near, far)
+        if last is not None:
+            got, _ = lax.optimization_barrier((got, last))
+        first, second = attend(low, heads, got, own, kept_key, kept_value)
+        last = second
+        results.append((low, handed(first, 1), handed(second, 0)))
+    out = None
+    for low, first, second in results:
+        out = unpack(low, order, first, second, out)
+    return out
 
 
 def per_device(query, key_new, value_new, stale_key, stale_value, head_order, tick):
@@ -316,6 +336,7 @@
     tok_rows, head_size = query.shape[1], stale_key.shape[3]
     paired = (
         group_size == 2
+        and lax.axis_size("segment") % 2 == 0
         and heads == 2 * stale_key.shape[1]
         and stale_key.shape[2] == MICRO * 2 * tok_rows
         and tok_rows % 16 == 0

time: 28.7 us -> 28.5 us (level)
  waiting for transfers between devices: 13.5 us -> 13.1 us
  Pallas kernels: 5.01 us -> 5.3 us
    pallas_call x2 -> x3, Pallas kernels: 1.96 us -> 2.59 us  [the longest x2 1.37 us: unpack(): pl.pallas_call(functools.partial(unpack_body, low), out_shape=pltpu.HBM(s...]
    ppermute x4, waiting for transfers between devices: 2.87 us -> 2.44 us  [handed(): return lax.ppermute(block, ('segment', 'seq'), route)]
    pallas_call x1, Pallas kernels: 1.75 us -> 1.42 us  [pack(): pl.pallas_call(functools.partial(pack_body, bounds), out_shape=shapes, in...]
  transfers between devices with their start and end apart: 6 -> 6, of which waited for: 3 -> 3; matrix products, arithmetic and copies ran while one was open for 0% -> 0% of each run, Pallas kernels for 9% -> 11%
where the time goes in v3:
time: 28.5 us; the launch traced here: 28.3 us
  waiting for transfers between devices  13.1 us (46%)
  starting transfers between devices  9.19 us (32%)
  Pallas kernels  5.3 us (19%)
  between operations  0.71 us (2%)
    ppermute x2, waiting for transfers between devices, pair_group(): received = [lax.ppermute(send, 'seq', [(0, 1), (1, 0)]) for send in sends]  10.6 us
    ppermute x4, starting transfers between devices, handed(): return lax.ppermute(block, ('segment', 'seq'), route)  6.08 us
    ppermute x2, starting transfers between devices, pair_group(): received = [lax.ppermute(send, 'seq', [(0, 1), (1, 0)]) for send in sends]  3.11 us
    ppermute x4, waiting for transfers between devices, handed(): return lax.ppermute(block, ('segment', 'seq'), route)  2.44 us
    pallas_call x1, Pallas kernels, pack(): pl.pallas_call(functools.partial(pack_body, bounds), out_shape=shapes, in...  1.42 us
    pallas_call x2, Pallas kernels, unpack(): pl.pallas_call(functools.partial(unpack_body, low), out_shape=pltpu.HBM(s...  1.37 us
    pallas_call x2, Pallas kernels, attend(): pl.pallas_call(functools.partial(attend_body, low), out_shape=(out, out),...  1.29 us
    pallas_call x1, Pallas kernels, keep(): pl.pallas_call(keep_body, out_shape=(own, kept, kept), in_specs=[scalar_s...  1.21 us
  transfers between devices with their start and end apart: 6, of which 3 were waited for; matrix products, arithmetic and copies ran while one was open for 0% of the time, Pallas kernels for 11%

profile of v3, /device:TPU:0, one launch (start us, length us, event | category | flops | bytes accessed | tf_op | source)
XLA Modules:
  0.0 28.3 jit_solution(6149229304972504624)
XLA Ops:
  0.0 1.4 %pack.1 = (s32[40]{0:T(128)S(4)}, bf16[3,48,5120]{2,1,0:T(8,128)(2,1)S(1)}, bf16[3,14,48,128]{3,2,1,0:T(8,128)(2,1)S(1)}, bf16[3,6,48,128]{3,2,1,0:T(8,128)(2,1)S(1)}) custom-call(s32[40]{0:T(128)} %given_ref.1, bf16[1,48,5120]{2,1,0:T(8,128)(2,1)} %query_ref.1, bf16[1,48,5120]{2,1,0:T(8,128)(2,1)} %key_ref.1, bf16[1,48,5120]{2,1,0:T(8,128)(2,1)} %value_ref.1), custom_call_target="tpu_custom_call" | custom-call | bytes 2949120 | tf_op jit(solution)/shard_map/pack/pallas_call | solution.py:165
  1.4 3.0 %collective-permute-start.1 = (bf16[3,14,48,128]{3,2,1,0:T(8,128)(2,1)S(1)}, bf16[3,14,48,128]{3,2,1,0:T(8,128)(2,1)S(1)}, u32[]{:S(2)}, u32[]{:S(2)}) collective-permute-start(bf16[3,14,48,128]{3,2,1,0:T(8,128)(2,1)S(1)} %get-tuple-element.19), channel_id=1, source_target_pairs={{0,4},{4,0},{1,5},{5,1},{2,6},{6,2},{3,7},{7,3},{8,12},{12,8},{9,1... | collective-permute-start | bytes 1548296 | tf_op jit(solution)/shard_map/ppermute | solution.py:318
  4.5 0.1 collective-permute-start
  5.2 1.2 %keep.1 = (bf16[3,20,48,128]{3,2,1,0:T(8,128)(2,1)S(1)}, bf16[20,96,128]{2,1,0:T(8,128)(2,1)S(1)}, bf16[20,96,128]{2,1,0:T(8,128)(2,1)S(1)}) custom-call(s32[40]{0:T(128)S(4)} %get-tuple-element.17.order_ref, s32[1]{0:T(128)S(6)} %copy.10.tick_ref, bf16[3,48,5120]{2,1,0:T(8,128)(2,1)S(1)} %get-tuple-element.20.fresh_ref, ...), custom_call_target="tpu_custom_call" | custom-call | bytes 1966080 | tf_op jit(solution)/shard_map/keep/pallas_call | solution.py:214
  6.4 10.6 %collective-permute-done.1.recv_ref = bf16[3,14,48,128]{3,2,1,0:T(8,128)(2,1)S(1)} collective-permute-done((bf16[3,14,48,128]{3,2,1,0:T(8,128)(2,1)S(1)}, bf16[3,14,48,128]{3,2,1,0:T(8,128)(2,1)S(1)}, u32[]{:S(2)}, u32[]{:S(2)}) %collective-permute-start.1) | collective-permute-done | bytes 516128 | tf_op jit(solution)/shard_map/ppermute | solution.py:318
  17.0 0.8 %attend.2 = (bf16[14,48,128]{2,1,0:T(8,128)(2,1)S(1)}, bf16[14,48,128]{2,1,0:T(8,128)(2,1)S(1)}) custom-call(bf16[3,14,48,128]{3,2,1,0:T(8,128)(2,1)S(1)} %collective-permute-done.1.recv_ref, bf16[3,20,48,128]{3,2,1,0:T(8,128)(2,1)S(1)} %get-tuple-element.21.own_ref, bf16[20,96,128]{2,1,0:T(8,128)(2,1)S(1)} %get-tuple-element.22.kept_key_ref, ...), custom_call_target="tpu_custom_call" | custom-call | flops 198180864 | bytes 2064384 | tf_op jit(solution)/shard_map/attend/pallas_call | solution.py:257
  17.8 0.1 collective-permute-start.4
  17.9 3.2 %collective-permute-start.5 = (bf16[14,48,128]{2,1,0:T(8,128)(2,1)S(1)}, bf16[14,48,128]{2,1,0:T(8,128)(2,1)S(1)}, u32[]{:S(2)}, u32[]{:S(2)}) collective-permute-start(bf16[14,48,128]{2,1,0:T(8,128)(2,1)S(1)} %get-tuple-element.24), channel_id=1, source_target_pairs={{0,12},{4,8},{8,16},{12,20},{16,28},{20,24},{24,0},{28,4},{1,13},{... | collective-permute-start | bytes 516104 | tf_op jit(solution)/shard_map/ppermute | solution.py:315
  21.1 0.0 collective-permute-done.recv_ref
  21.1 0.5 %attend.3 = (bf16[6,48,128]{2,1,0:T(8,128)(2,1)S(1)}, bf16[6,48,128]{2,1,0:T(8,128)(2,1)S(1)}) custom-call(bf16[3,6,48,128]{3,2,1,0:T(8,128)(2,1)S(1)} %collective-permute-done.recv_ref, bf16[3,20,48,128]{3,2,1,0:T(8,128)(2,1)S(1)} %get-tuple-element.21.own_ref, bf16[20,96,128]{2,1,0:T(8,128)(2,1)S(1)} %get-tuple-element.22.kept_key_ref, ...), custom_call_target="tpu_custom_call" | custom-call | flops 84934656 | bytes 884736 | tf_op jit(solution)/shard_map/attend/pallas_call | solution.py:257
  21.6 0.1 collective-permute-start.2
  21.7 2.8 %collective-permute-start.3 = (bf16[6,48,128]{2,1,0:T(8,128)(2,1)S(1)}, bf16[6,48,128]{2,1,0:T(8,128)(2,1)S(1)}, u32[]{:S(2)}, u32[]{:S(2)}) collective-permute-start(bf16[6,48,128]{2,1,0:T(8,128)(2,1)S(1)} %get-tuple-element.27), channel_id=1, source_target_pairs={{0,12},{4,8},{8,16},{12,20},{16,28},{20,24},{24,0},{28,4},{1,13},{... | collective-permute-start | bytes 221192 | tf_op jit(solution)/shard_map/ppermute | solution.py:315
  24.4 0.0 collective-permute-done.4.first_ref
  24.4 1.6 %collective-permute-done.5.second_ref = bf16[14,48,128]{2,1,0:T(8,128)(2,1)S(1)} collective-permute-done((bf16[14,48,128]{2,1,0:T(8,128)(2,1)S(1)}, bf16[14,48,128]{2,1,0:T(8,128)(2,1)S(1)}, u32[]{:S(2)}, u32[]{:S(2)}) %collective-permute-start.5) | collective-permute-done | bytes 172064 | tf_op jit(solution)/shard_map/ppermute | solution.py:315
  26.0 0.7 %unpack.2.refs_0_ = bf16[1,48,5120]{2,1,0:T(8,128)(2,1)} custom-call(s32[40]{0:T(128)S(4)} %get-tuple-element.17.order_ref, bf16[14,48,128]{2,1,0:T(8,128)(2,1)S(1)} %collective-permute-done.4.first_ref, bf16[14,48,128]{2,1,0:T(8,128)(2,1)S(1)} %collective-permute-done.5.second_ref), custom_call_target="tpu_custom_call" | custom-call | bytes 688128 | tf_op jit(solution)/shard_map/unpack/pallas_call | solution.py:287
  26.8 0.0 collective-permute-done.2.first_ref
  26.8 0.8 %collective-permute-done.3.second_ref = bf16[6,48,128]{2,1,0:T(8,128)(2,1)S(1)} collective-permute-done((bf16[6,48,128]{2,1,0:T(8,128)(2,1)S(1)}, bf16[6,48,128]{2,1,0:T(8,128)(2,1)S(1)}, u32[]{:S(2)}, u32[]{:S(2)}) %collective-permute-start.3) | collective-permute-done | bytes 73760 | tf_op jit(solution)/shard_map/ppermute | solution.py:315
  27.6 0.7 %unpack.3 = bf16[1,48,5120]{2,1,0:T(8,128)(2,1)} custom-call(s32[40]{0:T(128)S(4)} %get-tuple-element.17.order_ref, bf16[6,48,128]{2,1,0:T(8,128)(2,1)S(1)} %collective-permute-done.2.first_ref, bf16[6,48,128]{2,1,0:T(8,128)(2,1)S(1)} %collective-permute-done.3.second_ref, bf16[1,48,5120]{2,1,0:T(8,128)(2,1)} %unpack.2.refs_0_), custom_call_target="tpu_custom_call", output_to_operand_aliasing={{}: (3, {})} | custom-call | bytes 294912 | tf_op jit(solution)/shard_map/unpack/pallas_call | solution.py:287
Async XLA Ops:
  1.4 15.6 %collective-permute-start.1 = (bf16[3,14,48,128]{3,2,1,0:T(8,128)(2,1)S(1)}, bf16[3,14,48,128]{3,2,1,0:T(8,128)(2,1)S(1)}, u32[]{:S(2)}, u32[]{:S(2)}) collective-permute-start(bf16[3,14,48,128]{3,2,1,0:T(8,128)(2,1)S(1)} %get-tuple-element.19), channel_id=1, source_target_pairs={{0,4},{4,0},{1,5},{5,1},{2,6},{6,2},{3,7},{7,3},{8,12},{12,8},{9,1... | collective-permute-start | bytes 1548296 | tf_op jit(solution)/shard_map/ppermute | solution.py:318
  4.5 16.6 %collective-permute-start = (bf16[3,6,48,128]{3,2,1,0:T(8,128)(2,1)S(1)}, bf16[3,6,48,128]{3,2,1,0:T(8,128)(2,1)S(1)}, u32[]{:S(2)}, u32[]{:S(2)}) collective-permute-start(bf16[3,6,48,128]{3,2,1,0:T(8,128)(2,1)S(1)} %get-tuple-element.18), channel_id=1, source_target_pairs={{0,4},{4,0},{1,5},{5,1},{2,6},{6,2},{3,7},{7,3},{8,12},{12,8},{9,1... | collective-permute-start | bytes 663560 | tf_op jit(solution)/shard_map/ppermute | solution.py:318
  17.8 6.6 %collective-permute-start.4 = (bf16[14,48,128]{2,1,0:T(8,128)(2,1)S(1)}, bf16[14,48,128]{2,1,0:T(8,128)(2,1)S(1)}, u32[]{:S(2)}, u32[]{:S(2)}) collective-permute-start(bf16[14,48,128]{2,1,0:T(8,128)(2,1)S(1)} %get-tuple-element.28), channel_id=1, source_target_pairs={{0,8},{4,12},{8,20},{12,16},{16,24},{20,28},{24,4},{28,0},{1,9},{5... | collective-permute-start | bytes 516104 | tf_op jit(solution)/shard_map/ppermute | solution.py:315
  17.9 8.2 %collective-permute-start.5 = (bf16[14,48,128]{2,1,0:T(8,128)(2,1)S(1)}, bf16[14,48,128]{2,1,0:T(8,128)(2,1)S(1)}, u32[]{:S(2)}, u32[]{:S(2)}) collective-permute-start(bf16[14,48,128]{2,1,0:T(8,128)(2,1)S(1)} %get-tuple-element.24), channel_id=1, source_target_pairs={{0,12},{4,8},{8,16},{12,20},{16,28},{20,24},{24,0},{28,4},{1,13},{... | collective-permute-start | bytes 516104 | tf_op jit(solution)/shard_map/ppermute | solution.py:315
  21.6 5.1 %collective-permute-start.2 = (bf16[6,48,128]{2,1,0:T(8,128)(2,1)S(1)}, bf16[6,48,128]{2,1,0:T(8,128)(2,1)S(1)}, u32[]{:S(2)}, u32[]{:S(2)}) collective-permute-start(bf16[6,48,128]{2,1,0:T(8,128)(2,1)S(1)} %get-tuple-element.26), channel_id=1, source_target_pairs={{0,8},{4,12},{8,20},{12,16},{16,24},{20,28},{24,4},{28,0},{1,9},{5... | collective-permute-start | bytes 221192 | tf_op jit(solution)/shard_map/ppermute | solution.py:315
  21.7 5.9 %collective-permute-start.3 = (bf16[6,48,128]{2,1,0:T(8,128)(2,1)S(1)}, bf16[6,48,128]{2,1,0:T(8,128)(2,1)S(1)}, u32[]{:S(2)}, u32[]{:S(2)}) collective-permute-start(bf16[6,48,128]{2,1,0:T(8,128)(2,1)S(1)} %get-tuple-element.27), channel_id=1, source_target_pairs={{0,12},{4,8},{8,16},{12,20},{16,28},{20,24},{24,0},{28,4},{1,13},{... | collective-permute-start | bytes 221192 | tf_op jit(solution)/shard_map/ppermute | solution.py:315

commit v4 on v3

--- a/solution.py
+++ b/solution.py
@@ -8,7 +8,8 @@
 from jax.sharding import PartitionSpec as P
 
 MICRO = 2
-EDGES = (0, 0.7, 1)
+EARLY = 0.75
+RULE = (1, 0)
 KERNEL_VMEM = 8 << 20
 
 
@@ -134,50 +135,86 @@
     return pl.CostEstimate(flops=0, bytes_accessed=2 * count, transcendentals=0)
 
 
-def pack_body(bounds, given_ref, query_ref, key_ref, value_ref, order_ref, fresh_ref, *refs):
-    send_refs, (sems,) = refs[: len(bounds)], refs[len(bounds) :]
+def pack_pairs_body(
+    heads, given_ref, key_ref, value_ref, order_ref, pairs_ref, send_ref, sems
+):
     other = 1 - lax.axis_index("seq")
-    head_size = send_refs[0].shape[3]
+    head_size = send_ref.shape[3]
     copies = [
-        pltpu.make_async_copy(source.at[0], fresh_ref.at[place], sems.at[place])
-        for place, source in enumerate((key_ref, value_ref, query_ref))
-    ] + [pltpu.make_async_copy(given_ref, order_ref, sems.at[3])]
-    for copy in copies:
+        pltpu.make_async_copy(source_ref.at[0], pairs_ref.at[i], sems.at[i])
+        for i, source_ref in enumerate((key_ref, value_ref))
+    ]
+    order_copy = pltpu.make_async_copy(given_ref, order_ref, sems.at[2])
+    for copy in copies + [order_copy]:
         copy.start()
-    copies[3].wait()
-    for place in range(3):
-        copies[place].wait()
-        for (low, heads), send_ref in zip(bounds, send_refs):
-            for l in range(heads):
-                columns = columns_of(order_ref, 2 * (low + l) + other, head_size)
-                send_ref[place, l] = fresh_ref[place, :, columns]
-
-
-def pack(bounds, head_order, query, key_new, value_new):
+    order_copy.wait()
+    for i, copy in enumerate(copies):
+        copy.wait()
+        for l in range(heads):
+            send_ref[i, l] = pairs_ref[i, :, columns_of(order_ref, 2 * l + other, head_size)]
+
+
+def pack_pairs(heads, head_order, key_new, value_new):
+    tok_rows, width = key_new.shape[1:]
+    head_size = width // head_order.shape[0]
+    return pl.pallas_call(
+        functools.partial(pack_pairs_body, heads),
+        out_shape=(
+            pltpu.SMEM(head_order.shape, head_order.dtype),
+            jax.ShapeDtypeStruct((2, tok_rows, width), key_new.dtype),
+            jax.ShapeDtypeStruct((2, heads, tok_rows, head_size), key_new.dtype),
+        ),
+        in_specs=[hbm_space()] * 3,
+        out_specs=(scalar_space(), vmem_space(), vmem_space()),
+        scratch_shapes=[pltpu.SemaphoreType.DMA((3,))],
+        cost_estimate=moved(4 * tok_rows * width),
+        compiler_params=pltpu.CompilerParams(vmem_limit_bytes=KERNEL_VMEM),
+        name="pack_pairs",
+    )(in_hbm(head_order), in_hbm(key_new), in_hbm(value_new))
+
+
+def pack_rest_body(order_ref, pairs_ref, query_ref, fresh_ref, early_ref, late_ref, sem):
+    other = 1 - lax.axis_index("seq")
+    early, late = early_ref.shape[1], late_ref.shape[1]
+    head_size = early_ref.shape[3]
+    copy = pltpu.make_async_copy(query_ref.at[0], fresh_ref, sem)
+    copy.start()
+    for l in range(late):
+        columns = columns_of(order_ref, 2 * (early + l) + other, head_size)
+        for i in range(2):
+            late_ref[i, l] = pairs_ref[i, :, columns]
+    copy.wait()
+    for l in range(early + late):
+        columns = columns_of(order_ref, 2 * l + other, head_size)
+        if l < early:
+            early_ref[0, l] = fresh_ref[:, columns]
+        else:
+            late_ref[2, l - early] = fresh_ref[:, columns]
+
+
+def pack_rest(early, late, order, pairs, query):
     tok_rows, width = query.shape[1:]
-    head_size = width // head_order.shape[0]
-    shapes = [
-        pltpu.SMEM(head_order.shape, head_order.dtype),
-        jax.ShapeDtypeStruct((3, tok_rows, width), query.dtype),
-    ] + [
-        jax.ShapeDtypeStruct((3, heads, tok_rows, head_size), query.dtype) for _, heads in bounds
-    ]
-    order, fresh, *sends = pl.pallas_call(
-        functools.partial(pack_body, bounds),
-        out_shape=shapes,
-        in_specs=[hbm_space()] * 4,
-        out_specs=[scalar_space()] + [vmem_space()] * (len(shapes) - 1),
-        scratch_shapes=[pltpu.SemaphoreType.DMA((4,))],
-        cost_estimate=moved(6 * tok_rows * width),
+    head_size = width // order.shape[0]
+    return pl.pallas_call(
+        pack_rest_body,
+        out_shape=(
+            jax.ShapeDtypeStruct((tok_rows, width), query.dtype),
+            jax.ShapeDtypeStruct((1, early, tok_rows, head_size), query.dtype),
+            jax.ShapeDtypeStruct((3, late, tok_rows, head_size), query.dtype),
+        ),
+        in_specs=[scalar_space(), vmem_space(), hbm_space()],
+        out_specs=(vmem_space(),) * 3,
+        scratch_shapes=[pltpu.SemaphoreType.DMA],
+        cost_estimate=moved(2 * tok_rows * width),
         compiler_params=pltpu.CompilerParams(vmem_limit_bytes=KERNEL_VMEM),
-        name="pack",
-    )(*(in_hbm(x) for x in (head_order, query, key_new, value_new)))
-    return order, fresh, sends
+        name="pack_rest",
+    )(order, pairs, in_hbm(query))
 
 
 def keep_body(
     order_ref,
     tick_ref,
+    pairs_ref,
     fresh_ref,
     stale_key_ref,
     stale_value_ref,
@@ -201,92 +238,104 @@
         copy.start()
     for l in range(own_ref.shape[1]):
         columns = columns_of(order_ref, 2 * l + me, head_size)
-        for place in range(3):
-            own_ref[place, l] = fresh_ref[place, :, columns]
+        for i in range(2):
+            own_ref[i, l] = pairs_ref[i, :, columns]
+        own_ref[2, l] = fresh_ref[:, columns]
     for copy in copies:
         copy.wait()
 
 
-def keep(order, fresh, tick, stale_key, stale_value):
+def keep(order, pairs, fresh, tick, stale_key, stale_value):
     _, heads, length, head_size = stale_key.shape
-    own = jax.ShapeDtypeStruct((3, heads, fresh.shape[1], head_size), fresh.dtype)
+    own = jax.ShapeDtypeStruct((3, heads, fresh.shape[0], head_size), fresh.dtype)
     kept = jax.ShapeDtypeStruct((heads, length // MICRO, head_size), stale_key.dtype)
     return pl.pallas_call(
         keep_body,
         out_shape=(own, kept, kept),
-        in_specs=[scalar_space()] * 2 + [vmem_space()] + [hbm_space()] * 2,
+        in_specs=[scalar_space()] * 2 + [vmem_space()] * 2 + [hbm_space()] * 2,
         out_specs=(vmem_space(),) * 3,
         scratch_shapes=[pltpu.SemaphoreType.DMA((2,))],
         cost_estimate=moved(2 * heads * length * head_size),
         compiler_params=pltpu.CompilerParams(vmem_limit_bytes=KERNEL_VMEM),
         name="keep",
-    )(order, tick, fresh, in_hbm(stale_key), in_hbm(stale_value))
-
-
-def attend_body(low, recv_ref, own_ref, kept_key_ref, kept_value_ref, first_ref, second_ref):
-    odd = (lax.axis_index("segment") & 1) == 1
-    heads, tok_rows, head_size = first_ref.shape
+    )(order, tick, pairs, fresh, in_hbm(stale_key), in_hbm(stale_value))
+
+
+def crosses_first(section):
+    return jnp.where((section & 1) == 1, RULE[1], RULE[0])
+
+
+def attend_body(low, outs, recv_ref, query_ref, own_ref, kept_key_ref, kept_value_ref, *out_refs):
+    heads, tok_rows, head_size = out_refs[0].shape
+    dtype = out_refs[0].dtype
     factor = head_size ** (-0.5) * 1.4426950408889634
-    ones = jnp.ones((2 * kept_key_ref.shape[1], head_size), first_ref.dtype)
+    ones = jnp.ones((2 * kept_key_ref.shape[1], head_size), dtype)
+    turned = crosses_first(lax.axis_index("segment")) == 1
     for l in range(heads):
         at = low + l
         keys = jnp.concatenate([kept_key_ref[at], own_ref[0, at], recv_ref[0, l]], axis=0)
         values = jnp.concatenate([kept_value_ref[at], own_ref[1, at], recv_ref[1, l]], axis=0)
-        queries = jnp.concatenate([own_ref[2, at], recv_ref[2, l]], axis=0)
+        queries = {"near": lambda: own_ref[2, at], "far": lambda: query_ref[query_ref.shape[0] - 1, l]}
+        queries = jnp.concatenate([queries[out]() for out in outs], axis=0)
         scores = lax.dot_general(
             keys, queries, (((1,), (1,)), ((), ())), preferred_element_type=jnp.float32
         )
         top = jnp.max(scores, axis=0, keepdims=True)
-        weights = jnp.exp2((scores - top) * factor).astype(first_ref.dtype)
+        weights = jnp.exp2((scores - top) * factor).astype(dtype)
         both = lax.dot_general(
             weights,
             jnp.concatenate([values, ones], axis=1),
             (((0,), (0,)), ((), ())),
             preferred_element_type=jnp.float32,
         )
-        result = (both[:, :head_size] / both[:, head_size:]).astype(first_ref.dtype)
-        first_ref[l] = jnp.where(odd, result[tok_rows:], result[:tok_rows])
-        second_ref[l] = jnp.where(odd, result[:tok_rows], result[tok_rows:])
-
-
-def attend(low, heads, received, own, kept_key, kept_value):
+        result = (both[:, :head_size] / both[:, head_size:]).astype(dtype)
+        if len(outs) == 1:
+            out_refs[0][l] = result
+        else:
+            out_refs[0][l] = jnp.where(turned, result[tok_rows:], result[:tok_rows])
+            out_refs[1][l] = jnp.where(turned, result[:tok_rows], result[tok_rows:])
+
+
+def attend(low, heads, outs, received, queries, own, kept_key, kept_value):
     tok_rows, head_size = own.shape[2:]
-    patch_tok = 2 * tok_rows
-    length = MICRO * patch_tok
+    rows = len(outs) * tok_rows
+    length = 2 * MICRO * tok_rows
     out = jax.ShapeDtypeStruct((heads, tok_rows, head_size), own.dtype)
     return pl.pallas_call(
-        functools.partial(attend_body, low),
-        out_shape=(out, out),
-        in_specs=[vmem_space()] * 4,
-        out_specs=(vmem_space(),) * 2,
+        functools.partial(attend_body, low, outs),
+        out_shape=(out,) * len(outs),
+        in_specs=[vmem_space()] * 5,
+        out_specs=(vmem_space(),) * len(outs),
         cost_estimate=pl.CostEstimate(
-            flops=6 * heads * patch_tok * length * head_size,
-            bytes_accessed=2 * heads * head_size * (2 * length + 2 * patch_tok),
-            transcendentals=heads * patch_tok * length,
+            flops=6 * heads * rows * length * head_size,
+            bytes_accessed=2 * heads * head_size * (2 * length + 2 * rows),
+            transcendentals=heads * rows * length,
         ),
         compiler_params=pltpu.CompilerParams(vmem_limit_bytes=KERNEL_VMEM),
         name="attend",
-    )(received, own, kept_key, kept_value)
-
-
-def unpack_body(low, order_ref, first_ref, second_ref, *refs):
-    out_ref, sems = refs[-2:]
-    side = lax.axis_index("seq") ^ ((lax.axis_index("segment") + 1) & 1)
-    heads, _, head_size = first_ref.shape
+    )(received, queries, own, kept_key, kept_value)
+
+
+def unpack_body(low, turns, order_ref, *refs):
+    pieces, (out_ref, sems) = refs[:2], refs[-2:]
+    side = lax.axis_index("seq")
+    if turns:
+        side = side ^ crosses_first(lax.axis_index("segment") + 1)
+    heads, _, head_size = pieces[0].shape
     for l in range(heads):
-        for i, (owner, piece) in enumerate(((side, first_ref), (1 - side, second_ref))):
-            columns = columns_of(order_ref, 2 * (low + l) + owner, head_size)
+        for i, piece in enumerate(pieces):
+            columns = columns_of(order_ref, 2 * (low + l) + (side ^ i), head_size)
             pltpu.make_async_copy(piece.at[l], out_ref.at[0, :, columns], sems.at[i]).start()
-    for i, piece in enumerate((first_ref, second_ref)):
+    for i, piece in enumerate(pieces):
         pltpu.make_async_copy(piece, piece, sems.at[i]).wait()
 
 
-def unpack(low, order, first, second, out):
-    heads, tok_rows, head_size = first.shape
+def unpack(low, turns, order, pieces, out):
+    heads, tok_rows, head_size = pieces[0].shape
     shape = (1, tok_rows, order.shape[0] * head_size)
     return pl.pallas_call(
-        functools.partial(unpack_body, low),
-        out_shape=pltpu.HBM(shape, first.dtype),
+        functools.partial(unpack_body, low, turns),
+        out_shape=pltpu.HBM(shape, pieces[0].dtype),
         in_specs=[scalar_space()] + [vmem_space()] * 2 + [hbm_space()] * (out is not None),
         out_specs=hbm_space(),
         input_output_aliases={} if out is None else {3: 0},
@@ -294,40 +343,44 @@
         cost_estimate=moved(4 * heads * tok_rows * head_size),
         compiler_params=pltpu.CompilerParams(vmem_limit_bytes=KERNEL_VMEM),
         name="unpack",
-    )(order, first, second, *(() if out is None else (out,)))
-
-
-def chunks(heads_dev):
-    edges = [round(heads_dev * edge) for edge in EDGES]
-    return [(a, b - a) for a, b in zip(edges[:-1], edges[1:])]
+    )(order, *pieces, *(() if out is None else (out,)))
 
 
 def pair_group(query, key_new, value_new, stale_key, stale_value, head_order, tick):
     segments = lax.axis_size("segment")
-    bounds = chunks(stale_key.shape[1])
-
-    def handed(block, crossed):
+    heads_dev = stale_key.shape[1]
+    early = round(heads_dev * EARLY)
+    late = heads_dev - early
+
+    def swap(block):
+        return lax.ppermute(block, "seq", [(0, 1), (1, 0)])
+
+    def hand_on(block, rule):
         route = [
-            (2 * s + j, 2 * ((s + 1) % segments) + (1 - j if s % 2 == crossed else j))
+            (2 * s + j, 2 * ((s + 1) % segments) + (1 - j if rule[s % 2] else j))
             for s in range(segments)
             for j in range(2)
         ]
         return lax.ppermute(block, ("segment", "seq"), route)
 
-    order, fresh, sends = pack(bounds, head_order, query, key_new, value_new)
-    received = [lax.ppermute(send, "seq", [(0, 1), (1, 0)]) for send in sends]
-    own, kept_key, kept_value = keep(order, fresh, tick, stale_key, stale_value)
-    results, last = [], None
-    for (low, heads), got in zip(bounds, received):
-        if last is not None:
-            got, _ = lax.optimization_barrier((got, last))
-        first, second = attend(low, heads, got, own, kept_key, kept_value)
-        last = second
-        results.append((low, handed(first, 1), handed(second, 0)))
-    out = None
-    for low, first, second in results:
-        out = unpack(low, order, first, second, out)
-    return out
+    def after(block, other):
+        return lax.optimization_barrier((block, other))[0]
+
+    order, pairs, send = pack_pairs(early, head_order, key_new, value_new)
+    early_pairs = swap(send)
+    fresh, *sends = pack_rest(early, late, order, pairs, query)
+    early_queries, late_all = (swap(send) for send in sends)
+    held = keep(order, pairs, fresh, tick, stale_key, stale_value)
+    (near,) = attend(0, early, ("near",), early_pairs, early_pairs, *held)
+    near_early = hand_on(near, (0, 0))
+    early_queries = after(early_queries, near)
+    (far,) = attend(0, early, ("far",), early_pairs, early_queries, *held)
+    far_early = hand_on(far, (1, 1))
+    late_all = after(after(late_all, far), near_early)
+    first, second = attend(early, late, ("near", "far"), late_all, late_all, *held)
+    first, second = hand_on(first, RULE), hand_on(second, [1 - r for r in RULE])
+    out = unpack(0, False, order, (near_early, far_early), None)
+    return unpack(early, True, order, (first, second), out)
 
 
 def per_device(query, key_new, value_new, stale_key, stale_value, head_order, tick):

time: 28.5 us -> 27.8 us (0.975)
  starting transfers between devices: 9.19 us -> 7.21 us
  Pallas kernels: 5.3 us -> 6.89 us
  waiting for transfers between devices: 13.1 us -> 12.8 us
    ppermute x6 -> x7, starting transfers between devices: 9.19 us -> 7.21 us  [the longest x3 5.12 us: swap(): return lax.ppermute(block, 'seq', [(0, 1), (1, 0)])]
    pallas_call x5 -> x7, Pallas kernels: 4.09 us -> 5.68 us  [the longest x3 1.96 us: attend(): pl.pallas_call(functools.partial(attend_body, low, outs), out_shape=(out,...]
    ppermute x6 -> x7, waiting for transfers between devices: 13.1 us -> 12.8 us  [the longest x3 9.73 us: swap(): return lax.ppermute(block, 'seq', [(0, 1), (1, 0)])]
  transfers between devices with their start and end apart: 6 -> 7, of which waited for: 3 -> 6; matrix products, arithmetic and copies ran while one was open for 0% -> 0% of each run, Pallas kernels for 11% -> 18%
where the time goes in v4:
time: 27.8 us; the launch traced here: 27.6 us
  waiting for transfers between devices  12.8 us (46%)
  starting transfers between devices  7.21 us (26%)
  Pallas kernels  6.89 us (25%)
  between operations  0.72 us (3%)
    ppermute x3, waiting for transfers between devices, swap(): return lax.ppermute(block, 'seq', [(0, 1), (1, 0)])  9.73 us
    ppermute x3, starting transfers between devices, swap(): return lax.ppermute(block, 'seq', [(0, 1), (1, 0)])  5.12 us
    ppermute x4, waiting for transfers between devices, hand_on(): return lax.ppermute(block, ('segment', 'seq'), route)  3.03 us
    ppermute x4, starting transfers between devices, hand_on(): return lax.ppermute(block, ('segment', 'seq'), route)  2.09 us
    pallas_call x3, Pallas kernels, attend(): pl.pallas_call(functools.partial(attend_body, low, outs), out_shape=(out,...  1.96 us
    pallas_call x2, Pallas kernels, unpack(): pl.pallas_call(functools.partial(unpack_body, low, turns), out_shape=pltp...  1.37 us
    pallas_call x1, Pallas kernels, pack_pairs(): pl.pallas_call(functools.partial(pack_pairs_body, heads), out_shape=(pltp...  1.25 us
    pallas_call x1, Pallas kernels, keep(): pl.pallas_call(keep_body, out_shape=(own, kept, kept), in_specs=[scalar_s...  1.21 us
  transfers between devices with their start and end apart: 7, of which 6 were waited for; matrix products, arithmetic and copies ran while one was open for 0% of the time, Pallas kernels for 18%

profile of v4, /device:TPU:0, one launch (start us, length us, event | category | flops | bytes accessed | tf_op | source)
XLA Modules:
  0.0 27.6 jit_solution(4046986227478902798)
XLA Ops:
  0.0 1.3 %pack_pairs.1 = (s32[40]{0:T(128)S(4)}, bf16[2,48,5120]{2,1,0:T(8,128)(2,1)S(1)}, bf16[2,15,48,128]{3,2,1,0:T(8,128)(2,1)S(1)}) custom-call(s32[40]{0:T(128)} %given_ref.1, bf16[1,48,5120]{2,1,0:T(8,128)(2,1)} %key_ref.1, bf16[1,48,5120]{2,1,0:T(8,128)(2,1)} %value_ref.1), custom_call_target="tpu_custom_call" | custom-call | bytes 1966080 | tf_op jit(solution)/shard_map/pack_pairs/pallas_call | solution.py:160
  1.3 3.0 %collective-permute-start.1 = (bf16[2,15,48,128]{3,2,1,0:T(8,128)(2,1)S(1)}, bf16[2,15,48,128]{3,2,1,0:T(8,128)(2,1)S(1)}, u32[]{:S(2)}, u32[]{:S(2)}) collective-permute-start(bf16[2,15,48,128]{3,2,1,0:T(8,128)(2,1)S(1)} %get-tuple-element.22), channel_id=1, source_target_pairs={{0,4},{4,0},{1,5},{5,1},{2,6},{6,2},{3,7},{7,3},{8,12},{12,8},{9,1... | collective-permute-start | bytes 1105928 | tf_op jit(solution)/shard_map/ppermute | solution.py:356
  4.3 1.1 %pack_rest.1 = (bf16[48,5120]{1,0:T(8,128)(2,1)S(1)}, bf16[1,15,48,128]{3,2,1,0:T(8,128)(2,1)S(1)}, bf16[3,5,48,128]{3,2,1,0:T(8,128)(2,1)S(1)}) custom-call(s32[40]{0:T(128)S(4)} %get-tuple-element.19.order_ref, bf16[2,48,5120]{2,1,0:T(8,128)(2,1)S(1)} %get-tuple-element.20.pairs_ref, bf16[1,48,5120]{2,1,0:T(8,128)(2,1)} %query_ref.1), custom_call_target="tpu_custom_call" | custom-call | bytes 983040 | tf_op jit(solution)/shard_map/pack_rest/pallas_call | solution.py:198
  5.4 0.1 collective-permute-start.2
  5.5 2.0 %collective-permute-start = (bf16[3,5,48,128]{3,2,1,0:T(8,128)(2,1)S(1)}, bf16[3,5,48,128]{3,2,1,0:T(8,128)(2,1)S(1)}, u32[]{:S(2)}, u32[]{:S(2)}) collective-permute-start(bf16[3,5,48,128]{3,2,1,0:T(8,128)(2,1)S(1)} %get-tuple-element.21), channel_id=1, source_target_pairs={{0,4},{4,0},{1,5},{5,1},{2,6},{6,2},{3,7},{7,3},{8,12},{12,8},{9,1... | collective-permute-start | bytes 552968 | tf_op jit(solution)/shard_map/ppermute | solution.py:356
  8.1 1.2 %keep.1 = (bf16[3,20,48,128]{3,2,1,0:T(8,128)(2,1)S(1)}, bf16[20,96,128]{2,1,0:T(8,128)(2,1)S(1)}, bf16[20,96,128]{2,1,0:T(8,128)(2,1)S(1)}) custom-call(s32[40]{0:T(128)S(4)} %get-tuple-element.19.order_ref, s32[1]{0:T(128)S(6)} %copy.10.tick_ref, bf16[2,48,5120]{2,1,0:T(8,128)(2,1)S(1)} %get-tuple-element.20.pairs_ref, ...), custom_call_target="tpu_custom_call" | custom-call | bytes 1966080 | tf_op jit(solution)/shard_map/keep/pallas_call | solution.py:252
  9.4 4.3 %collective-permute-done.1.recv_ref.query_ref = bf16[2,15,48,128]{3,2,1,0:T(8,128)(2,1)S(1)} collective-permute-done((bf16[2,15,48,128]{3,2,1,0:T(8,128)(2,1)S(1)}, bf16[2,15,48,128]{3,2,1,0:T(8,128)(2,1)S(1)}, u32[]{:S(2)}, u32[]{:S(2)}) %collective-permute-start.1) | collective-permute-done | bytes 368672 | tf_op jit(solution)/shard_map/ppermute | solution.py:356
  13.7 0.7 %attend.3 = bf16[15,48,128]{2,1,0:T(8,128)(2,1)S(1)} custom-call(bf16[2,15,48,128]{3,2,1,0:T(8,128)(2,1)S(1)} %collective-permute-done.1.recv_ref.query_ref, bf16[2,15,48,128]{3,2,1,0:T(8,128)(2,1)S(1)} %collective-permute-done.1.recv_ref.query_ref, bf16[3,20,48,128]{3,2,1,0:T(8,128)(2,1)S(1)} %get-tuple-element.25.own_ref, ...), custom_call_target="tpu_custom_call" | custom-call | flops 106168320 | bytes 1843200 | tf_op jit(solution)/shard_map/attend/pallas_call | solution.py:304
  14.4 0.1 collective-permute-start.3
  14.5 3.2 %collective-permute-done.2.query_ref = bf16[1,15,48,128]{3,2,1,0:T(8,128)(2,1)S(1)} collective-permute-done((bf16[1,15,48,128]{3,2,1,0:T(8,128)(2,1)S(1)}, bf16[1,15,48,128]{3,2,1,0:T(8,128)(2,1)S(1)}, u32[]{:S(2)}, u32[]{:S(2)}) %collective-permute-start.2) | collective-permute-done | bytes 184352 | tf_op jit(solution)/shard_map/ppermute | solution.py:356
  17.7 0.7 %attend.4 = bf16[15,48,128]{2,1,0:T(8,128)(2,1)S(1)} custom-call(bf16[2,15,48,128]{3,2,1,0:T(8,128)(2,1)S(1)} %collective-permute-done.1.recv_ref.query_ref, bf16[1,15,48,128]{3,2,1,0:T(8,128)(2,1)S(1)} %collective-permute-done.2.query_ref, bf16[3,20,48,128]{3,2,1,0:T(8,128)(2,1)S(1)} %get-tuple-element.25.own_ref, ...), custom_call_target="tpu_custom_call" | custom-call | flops 106168320 | bytes 1843200 | tf_op jit(solution)/shard_map/attend/pallas_call | solution.py:304
  18.4 0.2 collective-permute-start.6
  18.5 2.2 %collective-permute-done.recv_ref.query_ref = bf16[3,5,48,128]{3,2,1,0:T(8,128)(2,1)S(1)} collective-permute-done((bf16[3,5,48,128]{3,2,1,0:T(8,128)(2,1)S(1)}, bf16[3,5,48,128]{3,2,1,0:T(8,128)(2,1)S(1)}, u32[]{:S(2)}, u32[]{:S(2)}) %collective-permute-start) | collective-permute-done | bytes 184352 | tf_op jit(solution)/shard_map/ppermute | solution.py:356
  20.8 0.0 collective-permute-done.3.refs_0_
  20.8 0.5 %attend.5 = (bf16[5,48,128]{2,1,0:T(8,128)(2,1)S(1)}, bf16[5,48,128]{2,1,0:T(8,128)(2,1)S(1)}) custom-call(bf16[3,5,48,128]{3,2,1,0:T(8,128)(2,1)S(1)} %collective-permute-done.recv_ref.query_ref, bf16[3,5,48,128]{3,2,1,0:T(8,128)(2,1)S(1)} %collective-permute-done.recv_ref.query_ref, bf16[3,20,48,128]{3,2,1,0:T(8,128)(2,1)S(1)} %get-tuple-element.25.own_ref, ...), custom_call_target="tpu_custom_call" | custom-call | flops 70778880 | bytes 737280 | tf_op jit(solution)/shard_map/attend/pallas_call | solution.py:304
  21.3 0.9 %collective-permute-start.4 = (bf16[5,48,128]{2,1,0:T(8,128)(2,1)S(1)}, bf16[5,48,128]{2,1,0:T(8,128)(2,1)S(1)}, u32[]{:S(2)}, u32[]{:S(2)}) collective-permute-start(bf16[5,48,128]{2,1,0:T(8,128)(2,1)S(1)} %get-tuple-element.31), channel_id=1, source_target_pairs={{0,12},{4,8},{8,16},{12,20},{16,28},{20,24},{24,0},{28,4},{1,13},{... | collective-permute-start | bytes 184328 | tf_op jit(solution)/shard_map/ppermute | solution.py:364
  22.2 0.9 %collective-permute-start.5 = (bf16[5,48,128]{2,1,0:T(8,128)(2,1)S(1)}, bf16[5,48,128]{2,1,0:T(8,128)(2,1)S(1)}, u32[]{:S(2)}, u32[]{:S(2)}) collective-permute-start(bf16[5,48,128]{2,1,0:T(8,128)(2,1)S(1)} %get-tuple-element.32), channel_id=1, source_target_pairs={{0,8},{4,12},{8,20},{12,16},{16,24},{20,28},{24,4},{28,0},{1,9},{5... | collective-permute-start | bytes 184328 | tf_op jit(solution)/shard_map/ppermute | solution.py:364
  23.2 1.2 %collective-permute-done.6.refs_1_ = bf16[15,48,128]{2,1,0:T(8,128)(2,1)S(1)} collective-permute-done((bf16[15,48,128]{2,1,0:T(8,128)(2,1)S(1)}, bf16[15,48,128]{2,1,0:T(8,128)(2,1)S(1)}, u32[]{:S(2)}, u32[]{:S(2)}) %collective-permute-start.6) | collective-permute-done | bytes 184352 | tf_op jit(solution)/shard_map/ppermute | solution.py:364
  24.4 0.7 %unpack.2.refs_2_ = bf16[1,48,5120]{2,1,0:T(8,128)(2,1)} custom-call(s32[40]{0:T(128)S(4)} %get-tuple-element.19.order_ref, bf16[15,48,128]{2,1,0:T(8,128)(2,1)S(1)} %collective-permute-done.3.refs_0_, bf16[15,48,128]{2,1,0:T(8,128)(2,1)S(1)} %collective-permute-done.6.refs_1_), custom_call_target="tpu_custom_call" | custom-call | bytes 737280 | tf_op jit(solution)/shard_map/unpack/pallas_call | solution.py:336
  25.1 0.5 %collective-permute-done.4.refs_0_ = bf16[5,48,128]{2,1,0:T(8,128)(2,1)S(1)} collective-permute-done((bf16[5,48,128]{2,1,0:T(8,128)(2,1)S(1)}, bf16[5,48,128]{2,1,0:T(8,128)(2,1)S(1)}, u32[]{:S(2)}, u32[]{:S(2)}) %collective-permute-start.4) | collective-permute-done | bytes 61472 | tf_op jit(solution)/shard_map/ppermute | solution.py:364
  25.6 1.3 %collective-permute-done.5.refs_1_ = bf16[5,48,128]{2,1,0:T(8,128)(2,1)S(1)} collective-permute-done((bf16[5,48,128]{2,1,0:T(8,128)(2,1)S(1)}, bf16[5,48,128]{2,1,0:T(8,128)(2,1)S(1)}, u32[]{:S(2)}, u32[]{:S(2)}) %collective-permute-start.5) | collective-permute-done | bytes 61472 | tf_op jit(solution)/shard_map/ppermute | solution.py:364
  26.9 0.6 %unpack.3 = bf16[1,48,5120]{2,1,0:T(8,128)(2,1)} custom-call(s32[40]{0:T(128)S(4)} %get-tuple-element.19.order_ref, bf16[5,48,128]{2,1,0:T(8,128)(2,1)S(1)} %collective-permute-done.4.refs_0_, bf16[5,48,128]{2,1,0:T(8,128)(2,1)S(1)} %collective-permute-done.5.refs_1_, bf16[1,48,5120]{2,1,0:T(8,128)(2,1)} %unpack.2.refs_2_), custom_call_target="tpu_custom_call", output_to_operand_aliasing={{}: (3, {})} | custom-call | bytes 245760 | tf_op jit(solution)/shard_map/unpack/pallas_call | solution.py:336
Async XLA Ops:
  1.3 12.4 %collective-permute-start.1 = (bf16[2,15,48,128]{3,2,1,0:T(8,128)(2,1)S(1)}, bf16[2,15,48,128]{3,2,1,0:T(8,128)(2,1)S(1)}, u32[]{:S(2)}, u32[]{:S(2)}) collective-permute-start(bf16[2,15,48,128]{3,2,1,0:T(8,128)(2,1)S(1)} %get-tuple-element.22), channel_id=1, source_target_pairs={{0,4},{4,0},{1,5},{5,1},{2,6},{6,2},{3,7},{7,3},{8,12},{12,8},{9,1... | collective-permute-start | bytes 1105928 | tf_op jit(solution)/shard_map/ppermute | solution.py:356
  5.4 12.3 %collective-permute-start.2 = (bf16[1,15,48,128]{3,2,1,0:T(8,128)(2,1)S(1)}, bf16[1,15,48,128]{3,2,1,0:T(8,128)(2,1)S(1)}, u32[]{:S(2)}, u32[]{:S(2)}) collective-permute-start(bf16[1,15,48,128]{3,2,1,0:T(8,128)(2,1)S(1)} %get-tuple-element.23), channel_id=1, source_target_pairs={{0,4},{4,0},{1,5},{5,1},{2,6},{6,2},{3,7},{7,3},{8,12},{12,8},{9,1... | collective-permute-start | bytes 552968 | tf_op jit(solution)/shard_map/ppermute | solution.py:356
  5.5 15.3 %collective-permute-start = (bf16[3,5,48,128]{3,2,1,0:T(8,128)(2,1)S(1)}, bf16[3,5,48,128]{3,2,1,0:T(8,128)(2,1)S(1)}, u32[]{:S(2)}, u32[]{:S(2)}) collective-permute-start(bf16[3,5,48,128]{3,2,1,0:T(8,128)(2,1)S(1)} %get-tuple-element.21), channel_id=1, source_target_pairs={{0,4},{4,0},{1,5},{5,1},{2,6},{6,2},{3,7},{7,3},{8,12},{12,8},{9,1... | collective-permute-start | bytes 552968 | tf_op jit(solution)/shard_map/ppermute | solution.py:356
  14.4 6.3 %collective-permute-start.3 = (bf16[15,48,128]{2,1,0:T(8,128)(2,1)S(1)}, bf16[15,48,128]{2,1,0:T(8,128)(2,1)S(1)}, u32[]{:S(2)}, u32[]{:S(2)}) collective-permute-start(bf16[15,48,128]{2,1,0:T(8,128)(2,1)S(1)} %attend.3), channel_id=1, source_target_pairs={{0,8},{4,12},{8,16},{12,20},{16,24},{20,28},{24,0},{28,4},{1,9},{5... | collective-permute-start | bytes 552968 | tf_op jit(solution)/shard_map/ppermute | solution.py:364
  18.4 6.0 %collective-permute-start.6 = (bf16[15,48,128]{2,1,0:T(8,128)(2,1)S(1)}, bf16[15,48,128]{2,1,0:T(8,128)(2,1)S(1)}, u32[]{:S(2)}, u32[]{:S(2)}) collective-permute-start(bf16[15,48,128]{2,1,0:T(8,128)(2,1)S(1)} %attend.4), channel_id=1, source_target_pairs={{0,12},{4,8},{8,20},{12,16},{16,28},{20,24},{24,4},{28,0},{1,13},{... | collective-permute-start | bytes 552968 | tf_op jit(solution)/shard_map/ppermute | solution.py:364
  21.3 4.3 %collective-permute-start.4 = (bf16[5,48,128]{2,1,0:T(8,128)(2,1)S(1)}, bf16[5,48,128]{2,1,0:T(8,128)(2,1)S(1)}, u32[]{:S(2)}, u32[]{:S(2)}) collective-permute-start(bf16[5,48,128]{2,1,0:T(8,128)(2,1)S(1)} %get-tuple-element.31), channel_id=1, source_target_pairs={{0,12},{4,8},{8,16},{12,20},{16,28},{20,24},{24,0},{28,4},{1,13},{... | collective-permute-start | bytes 184328 | tf_op jit(solution)/shard_map/ppermute | solution.py:364
  22.2 4.7 %collective-permute-start.5 = (bf16[5,48,128]{2,1,0:T(8,128)(2,1)S(1)}, bf16[5,48,128]{2,1,0:T(8,128)(2,1)S(1)}, u32[]{:S(2)}, u32[]{:S(2)}) collective-permute-start(bf16[5,48,128]{2,1,0:T(8,128)(2,1)S(1)} %get-tuple-element.32), channel_id=1, source_target_pairs={{0,8},{4,12},{8,20},{12,16},{16,24},{20,28},{24,4},{28,0},{1,9},{5... | collective-permute-start | bytes 184328 | tf_op jit(solution)/shard_map/ppermute | solution.py:364

commit v5 on v4

--- a/solution.py
+++ b/solution.py
@@ -135,86 +135,88 @@
     return pl.CostEstimate(flops=0, bytes_accessed=2 * count, transcendentals=0)
 
 
-def pack_pairs_body(
-    heads, given_ref, key_ref, value_ref, order_ref, pairs_ref, send_ref, sems
-):
+def pack_keys_body(given_ref, key_ref, order_ref, fresh_ref, send_ref, sems):
     other = 1 - lax.axis_index("seq")
-    head_size = send_ref.shape[3]
-    copies = [
-        pltpu.make_async_copy(source_ref.at[0], pairs_ref.at[i], sems.at[i])
-        for i, source_ref in enumerate((key_ref, value_ref))
-    ]
-    order_copy = pltpu.make_async_copy(given_ref, order_ref, sems.at[2])
-    for copy in copies + [order_copy]:
-        copy.start()
+    _, heads, _, head_size = send_ref.shape
+    order_copy = pltpu.make_async_copy(given_ref, order_ref, sems.at[1])
+    copy = pltpu.make_async_copy(key_ref.at[0], fresh_ref, sems.at[0])
+    copy.start()
+    order_copy.start()
     order_copy.wait()
-    for i, copy in enumerate(copies):
-        copy.wait()
-        for l in range(heads):
-            send_ref[i, l] = pairs_ref[i, :, columns_of(order_ref, 2 * l + other, head_size)]
-
-
-def pack_pairs(heads, head_order, key_new, value_new):
+    copy.wait()
+    for l in range(heads):
+        send_ref[0, l] = fresh_ref[:, columns_of(order_ref, 2 * l + other, head_size)]
+
+
+def pack_keys(heads, head_order, key_new):
     tok_rows, width = key_new.shape[1:]
     head_size = width // head_order.shape[0]
     return pl.pallas_call(
-        functools.partial(pack_pairs_body, heads),
+        pack_keys_body,
         out_shape=(
             pltpu.SMEM(head_order.shape, head_order.dtype),
-            jax.ShapeDtypeStruct((2, tok_rows, width), key_new.dtype),
-            jax.ShapeDtypeStruct((2, heads, tok_rows, head_size), key_new.dtype),
+            jax.ShapeDtypeStruct((tok_rows, width), key_new.dtype),
+            jax.ShapeDtypeStruct((1, heads, tok_rows, head_size), key_new.dtype),
         ),
-        in_specs=[hbm_space()] * 3,
+        in_specs=[hbm_space()] * 2,
         out_specs=(scalar_space(), vmem_space(), vmem_space()),
-        scratch_shapes=[pltpu.SemaphoreType.DMA((3,))],
-        cost_estimate=moved(4 * tok_rows * width),
+        scratch_shapes=[pltpu.SemaphoreType.DMA((2,))],
+        cost_estimate=moved(2 * tok_rows * width),
         compiler_params=pltpu.CompilerParams(vmem_limit_bytes=KERNEL_VMEM),
-        name="pack_pairs",
-    )(in_hbm(head_order), in_hbm(key_new), in_hbm(value_new))
-
-
-def pack_rest_body(order_ref, pairs_ref, query_ref, fresh_ref, early_ref, late_ref, sem):
+        name="pack_keys",
+    )(in_hbm(head_order), in_hbm(key_new))
+
+
+def pack_rest_body(
+    order_ref, keys_ref, value_ref, query_ref, fresh_ref, values_ref, queries_ref, late_ref, sems
+):
     other = 1 - lax.axis_index("seq")
-    early, late = early_ref.shape[1], late_ref.shape[1]
-    head_size = early_ref.shape[3]
-    copy = pltpu.make_async_copy(query_ref.at[0], fresh_ref, sem)
-    copy.start()
+    early, late = values_ref.shape[1], late_ref.shape[1]
+    head_size = late_ref.shape[3]
+    copies = [
+        pltpu.make_async_copy(source_ref.at[0], fresh_ref.at[i], sems.at[i])
+        for i, source_ref in enumerate((value_ref, query_ref))
+    ]
+    for copy in copies:
+        copy.start()
     for l in range(late):
         columns = columns_of(order_ref, 2 * (early + l) + other, head_size)
-        for i in range(2):
-            late_ref[i, l] = pairs_ref[i, :, columns]
-    copy.wait()
-    for l in range(early + late):
-        columns = columns_of(order_ref, 2 * l + other, head_size)
-        if l < early:
-            early_ref[0, l] = fresh_ref[:, columns]
-        else:
-            late_ref[2, l - early] = fresh_ref[:, columns]
-
-
-def pack_rest(early, late, order, pairs, query):
+        late_ref[0, l] = keys_ref[:, columns]
+    for i, target_ref in enumerate((values_ref, queries_ref)):
+        copies[i].wait()
+        for l in range(early + late):
+            columns = columns_of(order_ref, 2 * l + other, head_size)
+            if l < early:
+                target_ref[0, l] = fresh_ref[i, :, columns]
+            else:
+                late_ref[1 + i, l - early] = fresh_ref[i, :, columns]
+
+
+def pack_rest(early, late, order, keys, value_new, query):
     tok_rows, width = query.shape[1:]
     head_size = width // order.shape[0]
+    sent = jax.ShapeDtypeStruct((1, early, tok_rows, head_size), query.dtype)
     return pl.pallas_call(
         pack_rest_body,
         out_shape=(
-            jax.ShapeDtypeStruct((tok_rows, width), query.dtype),
-            jax.ShapeDtypeStruct((1, early, tok_rows, head_size), query.dtype),
+            jax.ShapeDtypeStruct((2, tok_rows, width), query.dtype),
+            sent,
+            sent,
             jax.ShapeDtypeStruct((3, late, tok_rows, head_size), query.dtype),
         ),
-        in_specs=[scalar_space(), vmem_space(), hbm_space()],
-        out_specs=(vmem_space(),) * 3,
-        scratch_shapes=[pltpu.SemaphoreType.DMA],
-        cost_estimate=moved(2 * tok_rows * width),
+        in_specs=[scalar_space(), vmem_space()] + [hbm_space()] * 2,
+        out_specs=(vmem_space(),) * 4,
+        scratch_shapes=[pltpu.SemaphoreType.DMA((2,))],
+        cost_estimate=moved(4 * tok_rows * width),
         compiler_params=pltpu.CompilerParams(vmem_limit_bytes=KERNEL_VMEM),
         name="pack_rest",
-    )(order, pairs, in_hbm(query))
+    )(order, keys, in_hbm(value_new), in_hbm(query))
 
 
 def keep_body(
     order_ref,
     tick_ref,
-    pairs_ref,
+    keys_ref,
     fresh_ref,
     stale_key_ref,
     stale_value_ref,
@@ -238,16 +240,16 @@
         copy.start()
     for l in range(own_ref.shape[1]):
         columns = columns_of(order_ref, 2 * l + me, head_size)
+        own_ref[0, l] = keys_ref[:, columns]
         for i in range(2):
-            own_ref[i, l] = pairs_ref[i, :, columns]
-        own_ref[2, l] = fresh_ref[:, columns]
+            own_ref[1 + i, l] = fresh_ref[i, :, columns]
     for copy in copies:
         copy.wait()
 
 
-def keep(order, pairs, fresh, tick, stale_key, stale_value):
+def keep(order, keys, fresh, tick, stale_key, stale_value):
     _, heads, length, head_size = stale_key.shape
-    own = jax.ShapeDtypeStruct((3, heads, fresh.shape[0], head_size), fresh.dtype)
+    own = jax.ShapeDtypeStruct((3, heads, fresh.shape[1], head_size), fresh.dtype)
     kept = jax.ShapeDtypeStruct((heads, length // MICRO, head_size), stale_key.dtype)
     return pl.pallas_call(
         keep_body,
@@ -258,14 +260,14 @@
         cost_estimate=moved(2 * heads * length * head_size),
         compiler_params=pltpu.CompilerParams(vmem_limit_bytes=KERNEL_VMEM),
         name="keep",
-    )(order, tick, pairs, fresh, in_hbm(stale_key), in_hbm(stale_value))
+    )(order, tick, keys, fresh, in_hbm(stale_key), in_hbm(stale_value))
 
 
 def crosses_first(section):
     return jnp.where((section & 1) == 1, RULE[1], RULE[0])
 
 
-def attend_body(low, outs, recv_ref, query_ref, own_ref, kept_key_ref, kept_value_ref, *out_refs):
+def attend_body(low, outs, recv_key_ref, recv_value_ref, query_ref, own_ref, kept_key_ref, kept_value_ref, *out_refs):
     heads, tok_rows, head_size = out_refs[0].shape
     dtype = out_refs[0].dtype
     factor = head_size ** (-0.5) * 1.4426950408889634
@@ -273,8 +275,8 @@
     turned = crosses_first(lax.axis_index("segment")) == 1
     for l in range(heads):
         at = low + l
-        keys = jnp.concatenate([kept_key_ref[at], own_ref[0, at], recv_ref[0, l]], axis=0)
-        values = jnp.concatenate([kept_value_ref[at], own_ref[1, at], recv_ref[1, l]], axis=0)
+        keys = jnp.concatenate([kept_key_ref[at], own_ref[0, at], recv_key_ref[0, l]], axis=0)
+        values = jnp.concatenate([kept_value_ref[at], own_ref[1, at], recv_value_ref[recv_value_ref.shape[0] // 2, l]], axis=0)
         queries = {"near": lambda: own_ref[2, at], "far": lambda: query_ref[query_ref.shape[0] - 1, l]}
         queries = jnp.concatenate([queries[out]() for out in outs], axis=0)
         scores = lax.dot_general(
@@ -296,7 +298,7 @@
             out_refs[1][l] = jnp.where(turned, result[:tok_rows], result[tok_rows:])
 
 
-def attend(low, heads, outs, received, queries, own, kept_key, kept_value):
+def attend(low, heads, outs, keys, values, queries, own, kept_key, kept_value):
     tok_rows, head_size = own.shape[2:]
     rows = len(outs) * tok_rows
     length = 2 * MICRO * tok_rows
@@ -304,7 +306,7 @@
     return pl.pallas_call(
         functools.partial(attend_body, low, outs),
         out_shape=(out,) * len(outs),
-        in_specs=[vmem_space()] * 5,
+        in_specs=[vmem_space()] * 6,
         out_specs=(vmem_space(),) * len(outs),
         cost_estimate=pl.CostEstimate(
             flops=6 * heads * rows * length * head_size,
@@ -313,7 +315,7 @@
         ),
         compiler_params=pltpu.CompilerParams(vmem_limit_bytes=KERNEL_VMEM),
         name="attend",
-    )(received, queries, own, kept_key, kept_value)
+    )(keys, values, queries, own, kept_key, kept_value)
 
 
 def unpack_body(low, turns, order_ref, *refs):
@@ -366,18 +368,19 @@
     def after(block, other):
         return lax.optimization_barrier((block, other))[0]
 
-    order, pairs, send = pack_pairs(early, head_order, key_new, value_new)
-    early_pairs = swap(send)
-    fresh, *sends = pack_rest(early, late, order, pairs, query)
-    early_queries, late_all = (swap(send) for send in sends)
-    held = keep(order, pairs, fresh, tick, stale_key, stale_value)
-    (near,) = attend(0, early, ("near",), early_pairs, early_pairs, *held)
+    order, keys, send = pack_keys(early, head_order, key_new)
+    early_keys = swap(send)
+    fresh, *sends = pack_rest(early, late, order, keys, value_new, query)
+    early_values, early_queries, late_all = (swap(send) for send in sends)
+    held = keep(order, keys, fresh, tick, stale_key, stale_value)
+    early_pairs = (early_keys, early_values)
+    (near,) = attend(0, early, ("near",), *early_pairs, early_values, *held)
     near_early = hand_on(near, (0, 0))
     early_queries = after(early_queries, near)
-    (far,) = attend(0, early, ("far",), early_pairs, early_queries, *held)
+    (far,) = attend(0, early, ("far",), *early_pairs, early_queries, *held)
     far_early = hand_on(far, (1, 1))
     late_all = after(after(late_all, far), near_early)
-    first, second = attend(early, late, ("near", "far"), late_all, late_all, *held)
+    first, second = attend(early, late, ("near", "far"), *[late_all] * 3, *held)
     first, second = hand_on(first, RULE), hand_on(second, [1 - r for r in RULE])
     out = unpack(0, False, order, (near_early, far_early), None)
     return unpack(early, True, order, (first, second), out)

time: 27.8 us -> 27.6 us (level)
  waiting for transfers between devices: 12.8 us -> 12.5 us
    ppermute x3 -> x4, waiting for transfers between devices: 9.73 us -> 9.48 us  [swap(): return lax.ppermute(block, 'seq', [(0, 1), (1, 0)])]
    ppermute x3 -> x4, starting transfers between devices: 5.12 us -> 5.2 us  [swap(): return lax.ppermute(block, 'seq', [(0, 1), (1, 0)])]
  transfers between devices with their start and end apart: 7 -> 8, of which waited for: 6 -> 7; matrix products, arithmetic and copies ran while one was open for 0% -> 0% of each run, Pallas kernels for 18% -> 19%
where the time goes in v5:
time: 27.6 us; the launch traced here: 27.4 us
  waiting for transfers between devices  12.5 us (45%)
  starting transfers between devices  7.29 us (26%)
  Pallas kernels  6.9 us (25%)
  between operations  0.72 us (3%)
    ppermute x4, waiting for transfers between devices, swap(): return lax.ppermute(block, 'seq', [(0, 1), (1, 0)])  9.48 us
    ppermute x4, starting transfers between devices, swap(): return lax.ppermute(block, 'seq', [(0, 1), (1, 0)])  5.2 us
    ppermute x4, waiting for transfers between devices, hand_on(): return lax.ppermute(block, ('segment', 'seq'), route)  3.03 us
    ppermute x4, starting transfers between devices, hand_on(): return lax.ppermute(block, ('segment', 'seq'), route)  2.09 us
    pallas_call x3, Pallas kernels, attend(): pl.pallas_call(functools.partial(attend_body, low, outs), out_shape=(out,...  1.96 us
    pallas_call x2, Pallas kernels, unpack(): pl.pallas_call(functools.partial(unpack_body, low, turns), out_shape=pltp...  1.37 us
    pallas_call x1, Pallas kernels, pack_rest(): pl.pallas_call(pack_rest_body, out_shape=(jax.ShapeDtypeStruct((2, tok_ro...  1.26 us
    pallas_call x1, Pallas kernels, keep(): pl.pallas_call(keep_body, out_shape=(own, kept, kept), in_specs=[scalar_s...  1.21 us
  transfers between devices with their start and end apart: 8, of which 7 were waited for; matrix products, arithmetic and copies ran while one was open for 0% of the time, Pallas kernels for 19%

profile of v5, /device:TPU:0, one launch (start us, length us, event | category | flops | bytes accessed | tf_op | source)
XLA Modules:
  0.0 27.4 jit_solution(16958260370217442642)
XLA Ops:
  0.0 1.1 %pack_keys.1 = (s32[40]{0:T(128)S(4)}, bf16[48,5120]{1,0:T(8,128)(2,1)S(1)}, bf16[1,15,48,128]{3,2,1,0:T(8,128)(2,1)S(1)}) custom-call(s32[40]{0:T(128)} %given_ref.1, bf16[1,48,5120]{2,1,0:T(8,128)(2,1)} %key_ref.1), custom_call_target="tpu_custom_call" | custom-call | bytes 983040 | tf_op jit(solution)/shard_map/pack_keys/pallas_call | solution.py:154
  1.1 3.0 %collective-permute-start.1 = (bf16[1,15,48,128]{3,2,1,0:T(8,128)(2,1)S(1)}, bf16[1,15,48,128]{3,2,1,0:T(8,128)(2,1)S(1)}, u32[]{:S(2)}, u32[]{:S(2)}) collective-permute-start(bf16[1,15,48,128]{3,2,1,0:T(8,128)(2,1)S(1)} %get-tuple-element.23), channel_id=1, source_target_pairs={{0,4},{4,0},{1,5},{5,1},{2,6},{6,2},{3,7},{7,3},{8,12},{12,8},{9,1... | collective-permute-start | bytes 552968 | tf_op jit(solution)/shard_map/ppermute | solution.py:358
  4.1 1.3 %pack_rest.1 = (bf16[2,48,5120]{2,1,0:T(8,128)(2,1)S(1)}, bf16[1,15,48,128]{3,2,1,0:T(8,128)(2,1)S(1)}, bf16[1,15,48,128]{3,2,1,0:T(8,128)(2,1)S(1)}, bf16[3,5,48,128]{3,2,1,0:T(8,128)(2,1)S(1)}) custom-call(s32[40]{0:T(128)S(4)} %get-tuple-element.20.order_ref, bf16[48,5120]{1,0:T(8,128)(2,1)S(1)} %get-tuple-element.21.keys_ref, ...), custom_call_target="tpu_custom_call" | custom-call | bytes 1966080 | tf_op jit(solution)/shard_map/pack_rest/pallas_call | solution.py:199
  5.4 0.1 collective-permute-start.2
  5.5 2.0 %collective-permute-start.3 = (bf16[1,15,48,128]{3,2,1,0:T(8,128)(2,1)S(1)}, bf16[1,15,48,128]{3,2,1,0:T(8,128)(2,1)S(1)}, u32[]{:S(2)}, u32[]{:S(2)}) collective-permute-start(bf16[1,15,48,128]{3,2,1,0:T(8,128)(2,1)S(1)} %get-tuple-element.25), channel_id=1, source_target_pairs={{0,4},{4,0},{1,5},{5,1},{2,6},{6,2},{3,7},{7,3},{8,12},{12,8},{9,1... | collective-permute-start | bytes 552968 | tf_op jit(solution)/shard_map/ppermute | solution.py:358
  7.5 0.1 collective-permute-start
  8.2 1.2 %keep.1 = (bf16[3,20,48,128]{3,2,1,0:T(8,128)(2,1)S(1)}, bf16[20,96,128]{2,1,0:T(8,128)(2,1)S(1)}, bf16[20,96,128]{2,1,0:T(8,128)(2,1)S(1)}) custom-call(s32[40]{0:T(128)S(4)} %get-tuple-element.20.order_ref, s32[1]{0:T(128)S(6)} %copy.10.tick_ref, bf16[48,5120]{1,0:T(8,128)(2,1)S(1)} %get-tuple-element.21.keys_ref, ...), custom_call_target="tpu_custom_call" | custom-call | bytes 1966080 | tf_op jit(solution)/shard_map/keep/pallas_call | solution.py:254
  9.4 0.2 collective-permute-done.1.recv_key_ref
  9.6 3.9 %collective-permute-done.2.recv_value_ref.query_ref = bf16[1,15,48,128]{3,2,1,0:T(8,128)(2,1)S(1)} collective-permute-done((bf16[1,15,48,128]{3,2,1,0:T(8,128)(2,1)S(1)}, bf16[1,15,48,128]{3,2,1,0:T(8,128)(2,1)S(1)}, u32[]{:S(2)}, u32[]{:S(2)}) %collective-permute-start.2) | collective-permute-done | bytes 184352 | tf_op jit(solution)/shard_map/ppermute | solution.py:358
  13.6 0.7 %attend.3 = bf16[15,48,128]{2,1,0:T(8,128)(2,1)S(1)} custom-call(bf16[1,15,48,128]{3,2,1,0:T(8,128)(2,1)S(1)} %collective-permute-done.1.recv_key_ref, bf16[1,15,48,128]{3,2,1,0:T(8,128)(2,1)S(1)} %collective-permute-done.2.recv_value_ref.query_ref, bf16[1,15,48,128]{3,2,1,0:T(8,128)(2,1)S(1)} %collective-permute-done.2.recv_value_ref.query_ref, ...), custom_call_target="tpu_custom_call" | custom-call | flops 106168320 | bytes 1843200 | tf_op jit(solution)/shard_map/attend/pallas_call | solution.py:306
  14.3 0.1 collective-permute-start.4
  14.3 3.2 %collective-permute-done.3.query_ref = bf16[1,15,48,128]{3,2,1,0:T(8,128)(2,1)S(1)} collective-permute-done((bf16[1,15,48,128]{3,2,1,0:T(8,128)(2,1)S(1)}, bf16[1,15,48,128]{3,2,1,0:T(8,128)(2,1)S(1)}, u32[]{:S(2)}, u32[]{:S(2)}) %collective-permute-start.3) | collective-permute-done | bytes 184352 | tf_op jit(solution)/shard_map/ppermute | solution.py:358
  17.5 0.7 %attend.4 = bf16[15,48,128]{2,1,0:T(8,128)(2,1)S(1)} custom-call(bf16[1,15,48,128]{3,2,1,0:T(8,128)(2,1)S(1)} %collective-permute-done.1.recv_key_ref, bf16[1,15,48,128]{3,2,1,0:T(8,128)(2,1)S(1)} %collective-permute-done.2.recv_value_ref.query_ref, bf16[1,15,48,128]{3,2,1,0:T(8,128)(2,1)S(1)} %collective-permute-done.3.query_ref, ...), custom_call_target="tpu_custom_call" | custom-call | flops 106168320 | bytes 1843200 | tf_op jit(solution)/shard_map/attend/pallas_call | solution.py:306
  18.2 0.2 collective-permute-start.7
  18.4 2.2 %collective-permute-done.recv_key_ref.recv_value_ref.query_ref = bf16[3,5,48,128]{3,2,1,0:T(8,128)(2,1)S(1)} collective-permute-done((bf16[3,5,48,128]{3,2,1,0:T(8,128)(2,1)S(1)}, bf16[3,5,48,128]{3,2,1,0:T(8,128)(2,1)S(1)}, u32[]{:S(2)}, u32[]{:S(2)}) %collective-permute-start) | collective-permute-done | bytes 184352 | tf_op jit(solution)/shard_map/ppermute | solution.py:358
  20.6 0.0 collective-permute-done.4.refs_0_
  20.6 0.5 %attend.5 = (bf16[5,48,128]{2,1,0:T(8,128)(2,1)S(1)}, bf16[5,48,128]{2,1,0:T(8,128)(2,1)S(1)}) custom-call(bf16[3,5,48,128]{3,2,1,0:T(8,128)(2,1)S(1)} %collective-permute-done.recv_key_ref.recv_value_ref.query_ref, bf16[3,5,48,128]{3,2,1,0:T(8,128)(2,1)S(1)} %collective-permute-done.recv_key_ref.recv_value_ref.query_ref, ...), custom_call_target="tpu_custom_call" | custom-call | flops 70778880 | bytes 737280 | tf_op jit(solution)/shard_map/attend/pallas_call | solution.py:306
  21.1 0.9 %collective-permute-start.5 = (bf16[5,48,128]{2,1,0:T(8,128)(2,1)S(1)}, bf16[5,48,128]{2,1,0:T(8,128)(2,1)S(1)}, u32[]{:S(2)}, u32[]{:S(2)}) collective-permute-start(bf16[5,48,128]{2,1,0:T(8,128)(2,1)S(1)} %get-tuple-element.33), channel_id=1, source_target_pairs={{0,12},{4,8},{8,16},{12,20},{16,28},{20,24},{24,0},{28,4},{1,13},{... | collective-permute-start | bytes 184328 | tf_op jit(solution)/shard_map/ppermute | solution.py:366
  22.1 0.9 %collective-permute-start.6 = (bf16[5,48,128]{2,1,0:T(8,128)(2,1)S(1)}, bf16[5,48,128]{2,1,0:T(8,128)(2,1)S(1)}, u32[]{:S(2)}, u32[]{:S(2)}) collective-permute-start(bf16[5,48,128]{2,1,0:T(8,128)(2,1)S(1)} %get-tuple-element.34), channel_id=1, source_target_pairs={{0,8},{4,12},{8,20},{12,16},{16,24},{20,28},{24,4},{28,0},{1,9},{5... | collective-permute-start | bytes 184328 | tf_op jit(solution)/shard_map/ppermute | solution.py:366
  23.0 1.2 %collective-permute-done.7.refs_1_ = bf16[15,48,128]{2,1,0:T(8,128)(2,1)S(1)} collective-permute-done((bf16[15,48,128]{2,1,0:T(8,128)(2,1)S(1)}, bf16[15,48,128]{2,1,0:T(8,128)(2,1)S(1)}, u32[]{:S(2)}, u32[]{:S(2)}) %collective-permute-start.7) | collective-permute-done | bytes 184352 | tf_op jit(solution)/shard_map/ppermute | solution.py:366
  24.3 0.7 %unpack.2.refs_2_ = bf16[1,48,5120]{2,1,0:T(8,128)(2,1)} custom-call(s32[40]{0:T(128)S(4)} %get-tuple-element.20.order_ref, bf16[15,48,128]{2,1,0:T(8,128)(2,1)S(1)} %collective-permute-done.4.refs_0_, bf16[15,48,128]{2,1,0:T(8,128)(2,1)S(1)} %collective-permute-done.7.refs_1_), custom_call_target="tpu_custom_call" | custom-call | bytes 737280 | tf_op jit(solution)/shard_map/unpack/pallas_call | solution.py:338
  25.0 0.5 %collective-permute-done.5.refs_0_ = bf16[5,48,128]{2,1,0:T(8,128)(2,1)S(1)} collective-permute-done((bf16[5,48,128]{2,1,0:T(8,128)(2,1)S(1)}, bf16[5,48,128]{2,1,0:T(8,128)(2,1)S(1)}, u32[]{:S(2)}, u32[]{:S(2)}) %collective-permute-start.5) | collective-permute-done | bytes 61472 | tf_op jit(solution)/shard_map/ppermute | solution.py:366
  25.5 1.3 %collective-permute-done.6.refs_1_ = bf16[5,48,128]{2,1,0:T(8,128)(2,1)S(1)} collective-permute-done((bf16[5,48,128]{2,1,0:T(8,128)(2,1)S(1)}, bf16[5,48,128]{2,1,0:T(8,128)(2,1)S(1)}, u32[]{:S(2)}, u32[]{:S(2)}) %collective-permute-start.6) | collective-permute-done | bytes 61472 | tf_op jit(solution)/shard_map/ppermute | solution.py:366
  26.8 0.6 %unpack.3 = bf16[1,48,5120]{2,1,0:T(8,128)(2,1)} custom-call(s32[40]{0:T(128)S(4)} %get-tuple-element.20.order_ref, bf16[5,48,128]{2,1,0:T(8,128)(2,1)S(1)} %collective-permute-done.5.refs_0_, bf16[5,48,128]{2,1,0:T(8,128)(2,1)S(1)} %collective-permute-done.6.refs_1_, bf16[1,48,5120]{2,1,0:T(8,128)(2,1)} %unpack.2.refs_2_), custom_call_target="tpu_custom_call", output_to_operand_aliasing={{}: (3, {})} | custom-call | bytes 245760 | tf_op jit(solution)/shard_map/unpack/pallas_call | solution.py:338
Async XLA Ops:
  1.1 8.5 %collective-permute-start.1 = (bf16[1,15,48,128]{3,2,1,0:T(8,128)(2,1)S(1)}, bf16[1,15,48,128]{3,2,1,0:T(8,128)(2,1)S(1)}, u32[]{:S(2)}, u32[]{:S(2)}) collective-permute-start(bf16[1,15,48,128]{3,2,1,0:T(8,128)(2,1)S(1)} %get-tuple-element.23), channel_id=1, source_target_pairs={{0,4},{4,0},{1,5},{5,1},{2,6},{6,2},{3,7},{7,3},{8,12},{12,8},{9,1... | collective-permute-start | bytes 552968 | tf_op jit(solution)/shard_map/ppermute | solution.py:358
  5.4 8.2 %collective-permute-start.2 = (bf16[1,15,48,128]{3,2,1,0:T(8,128)(2,1)S(1)}, bf16[1,15,48,128]{3,2,1,0:T(8,128)(2,1)S(1)}, u32[]{:S(2)}, u32[]{:S(2)}) collective-permute-start(bf16[1,15,48,128]{3,2,1,0:T(8,128)(2,1)S(1)} %get-tuple-element.24), channel_id=1, source_target_pairs={{0,4},{4,0},{1,5},{5,1},{2,6},{6,2},{3,7},{7,3},{8,12},{12,8},{9,1... | collective-permute-start | bytes 552968 | tf_op jit(solution)/shard_map/ppermute | solution.py:358
  5.5 12.0 %collective-permute-start.3 = (bf16[1,15,48,128]{3,2,1,0:T(8,128)(2,1)S(1)}, bf16[1,15,48,128]{3,2,1,0:T(8,128)(2,1)S(1)}, u32[]{:S(2)}, u32[]{:S(2)}) collective-permute-start(bf16[1,15,48,128]{3,2,1,0:T(8,128)(2,1)S(1)} %get-tuple-element.25), channel_id=1, source_target_pairs={{0,4},{4,0},{1,5},{5,1},{2,6},{6,2},{3,7},{7,3},{8,12},{12,8},{9,1... | collective-permute-start | bytes 552968 | tf_op jit(solution)/shard_map/ppermute | solution.py:358
  7.5 13.1 %collective-permute-start = (bf16[3,5,48,128]{3,2,1,0:T(8,128)(2,1)S(1)}, bf16[3,5,48,128]{3,2,1,0:T(8,128)(2,1)S(1)}, u32[]{:S(2)}, u32[]{:S(2)}) collective-permute-start(bf16[3,5,48,128]{3,2,1,0:T(8,128)(2,1)S(1)} %get-tuple-element.22), channel_id=1, source_target_pairs={{0,4},{4,0},{1,5},{5,1},{2,6},{6,2},{3,7},{7,3},{8,12},{12,8},{9,1... | collective-permute-start | bytes 552968 | tf_op jit(solution)/shard_map/ppermute | solution.py:358
  14.3 6.3 %collective-permute-start.4 = (bf16[15,48,128]{2,1,0:T(8,128)(2,1)S(1)}, bf16[15,48,128]{2,1,0:T(8,128)(2,1)S(1)}, u32[]{:S(2)}, u32[]{:S(2)}) collective-permute-start(bf16[15,48,128]{2,1,0:T(8,128)(2,1)S(1)} %attend.3), channel_id=1, source_target_pairs={{0,8},{4,12},{8,16},{12,20},{16,24},{20,28},{24,0},{28,4},{1,9},{5... | collective-permute-start | bytes 552968 | tf_op jit(solution)/shard_map/ppermute | solution.py:366
  18.2 6.0 %collective-permute-start.7 = (bf16[15,48,128]{2,1,0:T(8,128)(2,1)S(1)}, bf16[15,48,128]{2,1,0:T(8,128)(2,1)S(1)}, u32[]{:S(2)}, u32[]{:S(2)}) collective-permute-start(bf16[15,48,128]{2,1,0:T(8,128)(2,1)S(1)} %attend.4), channel_id=1, source_target_pairs={{0,12},{4,8},{8,20},{12,16},{16,28},{20,24},{24,4},{28,0},{1,13},{... | collective-permute-start | bytes 552968 | tf_op jit(solution)/shard_map/ppermute | solution.py:366
  21.1 4.3 %collective-permute-start.5 = (bf16[5,48,128]{2,1,0:T(8,128)(2,1)S(1)}, bf16[5,48,128]{2,1,0:T(8,128)(2,1)S(1)}, u32[]{:S(2)}, u32[]{:S(2)}) collective-permute-start(bf16[5,48,128]{2,1,0:T(8,128)(2,1)S(1)} %get-tuple-element.33), channel_id=1, source_target_pairs={{0,12},{4,8},{8,16},{12,20},{16,28},{20,24},{24,0},{28,4},{1,13},{... | collective-permute-start | bytes 184328 | tf_op jit(solution)/shard_map/ppermute | solution.py:366
  22.1 4.7 %collective-permute-start.6 = (bf16[5,48,128]{2,1,0:T(8,128)(2,1)S(1)}, bf16[5,48,128]{2,1,0:T(8,128)(2,1)S(1)}, u32[]{:S(2)}, u32[]{:S(2)}) collective-permute-start(bf16[5,48,128]{2,1,0:T(8,128)(2,1)S(1)} %get-tuple-element.34), channel_id=1, source_target_pairs={{0,8},{4,12},{8,20},{12,16},{16,24},{20,28},{24,4},{28,0},{1,9},{5... | collective-permute-start | bytes 184328 | tf_op jit(solution)/shard_map/ppermute | solution.py:366
